TPU v7x, 256 devices: a whole 4x4x8 slice. The times are simulated.
256 devices in a mesh: row: 16 (over x, z_lo), col: 8 (over y, z_hi), ch: 2 (over core).
Axes of the slice: x: 4, y: 4, z: 8 (z_hi: 2, z_lo: 4; z = z_hi * 4 + z_lo), core: 2. Of those that a mesh axis runs over, the one named last changes fastest.
Arguments:
- pair: bfloat16 [384, 384, 128], P('row', 'col'), may hold values from -6 to 6
- cotangent: bfloat16 [384, 384, 128], P('row', 'col', 'ch'), may hold values from -6 to 6
- w_gate_a: bfloat16 [128, 128], P(None, 'ch'), may hold values from -0.5 to 0.5
- w_proj_a: bfloat16 [128, 128], P(None, 'ch'), may hold values from -0.5 to 0.5
- w_gate_b: bfloat16 [128, 128], P(None, 'ch'), may hold values from -0.5 to 0.5
- w_proj_b: bfloat16 [128, 128], P(None, 'ch'), may hold values from -0.5 to 0.5
- w_gate_out: bfloat16 [128, 128], P(None, 'ch'), may hold values from -0.5 to 0.5
- w_out: bfloat16 [128, 128], P(None, 'ch'), may hold values from -0.5 to 0.5
Outputs:
- updated: bfloat16 [384, 384, 128], P('row', 'col', 'ch')
- grad_pair: bfloat16 [384, 384, 128], P('row', 'col', 'ch')
- grad_gate_a: float32 [128, 128], P(None, 'ch')
- grad_proj_a: float32 [128, 128], P(None, 'ch')
- grad_gate_b: float32 [128, 128], P(None, 'ch')
- grad_proj_b: float32 [128, 128], P(None, 'ch')
- grad_gate_out: float32 [128, 128], P(None, 'ch')
- grad_out: float32 [128, 128], P(None, 'ch')
All inputs are finite; a program needn't handle non-finite values.
Results may differ from a plain program's by a relative error of at most 0.022.
Values may be sent and summed in bfloat16 or wider, within the bound.
A program may use at most 64 MiB of HBM per device.

v0:
```python
import jax
import jax.numpy as jnp
from jax import lax
from jax.experimental import pallas as pl
from jax.experimental.pallas import tpu as pltpu
from jax.sharding import PartitionSpec as P

MESH = pl.DeviceIdType.MESH
epsilon = 1e-05
f32, bf16 = jnp.float32, jnp.bfloat16
PAIRS, CHUNKS, LANES = 1152, 9, 128


def nn(a, b):
    return lax.dot_general(a, b, (((1,), (0,)), ((), ())), preferred_element_type=f32)


def nt(a, b):
    return lax.dot_general(a, b, (((1,), (1,)), ((), ())), preferred_element_type=f32)


def tn(a, b):
    return lax.dot_general(a, b, (((0,), (0,)), ((), ())), preferred_element_type=f32)


def sigmoid(x):
    return 1.0 / (1.0 + jnp.exp(-x))


def block_transpose(x):
    groups = x.shape[0] // 8
    x = x.reshape(groups, 8, 384)
    row = lax.broadcasted_iota(jnp.int32, x.shape, 1)
    part = lax.broadcasted_iota(jnp.int32, x.shape, 2) // 48
    for bit in (1, 2, 4):
        low = (row & bit) == 0
        same = low == ((part & bit) == 0)
        up = pltpu.roll(pltpu.roll(x, bit, 1), 384 - 48 * bit, 2)
        down = pltpu.roll(pltpu.roll(x, 8 - bit, 1), 48 * bit, 2)
        x = jnp.where(same, x, jnp.where(low, down, up))
    return x.reshape(groups * 8, 384)


def kernel(
    pair_ref, cot_ref, wga_ref, wpa_ref, wgb_ref, wpb_ref, wgo_ref, wo_ref,
    updated_ref, grad_ref, g0_ref, g1_ref, g2_ref, g3_ref, g4_ref, g5_ref,
    normed, hat, rstd1, acts, flat,
    send1, recv1, send2, recv2, send3, recv3, send4, recv4, send5, recv5, send6, recv6,
    left, right, dr_send, dr_recv, df_send, df_recv, part_send, part_recv,
    wgo_other, wo_other, cot_t, cot_other, gate_out, dproj, dgate, mixn, dfour,
    send_sem, recv_sem, psend_sem, precv_sem,
):
    row, col, ch = lax.axis_index("row"), lax.axis_index("col"), lax.axis_index("ch")
    slot = (row % 8) * 8 + col
    half = row // 8
    own = half == ch
    other = (row, col, 1 - ch)

    def peer(t):
        return (8 * ch + t // 8, t % 8, half)

    barrier = pltpu.get_barrier_semaphore()
    pl.semaphore_signal(barrier, inc=1, device_id=other, device_id_type=MESH)

    @pl.loop(1, 64)
    def _(k):
        pl.semaphore_signal(barrier, inc=1, device_id=peer((slot + k) % 64), device_id_type=MESH)

    @pl.when(jnp.logical_not(own))
    def _():
        pl.semaphore_signal(barrier, inc=1, device_id=peer(slot), device_id_type=MESH)

    def swap_start(n, src, dst, one=False):
        def at(t):
            return src if one else src.at[t]

        def copy(t):
            return pltpu.make_async_remote_copy(
                src_ref=at(t),
                dst_ref=dst.at[slot],
                send_sem=send_sem.at[n],
                recv_sem=recv_sem.at[n],
                device_id=peer(t),
                device_id_type=MESH,
            )

        @pl.when(own)
        def _():
            pltpu.make_async_copy(at(slot), dst.at[slot], recv_sem.at[n]).start()

        @pl.when(jnp.logical_not(own))
        def _():
            copy(slot).start()

        @pl.loop(1, 64)
        def _(k):
            copy((slot + k) % 64).start()

    def swap_wait(n, dst):
        pltpu.make_async_copy(dst, dst, recv_sem.at[n]).wait()

    def swap_drain(n, dst):
        @pl.when(own)
        def _():
            some = dst.at[pl.ds(0, 63)]
            pltpu.make_async_copy(some, some, send_sem.at[n]).wait()

        @pl.when(jnp.logical_not(own))
        def _():
            pltpu.make_async_copy(dst, dst, send_sem.at[n]).wait()

    def partner(n, src, dst):
        return pltpu.make_async_remote_copy(
            src_ref=src,
            dst_ref=dst,
            send_sem=psend_sem.at[n],
            recv_sem=precv_sem.at[n],
            device_id=other,
            device_id_type=MESH,
        )

    def put(t_rows, g, value):
        flat[pl.ds(g, 64, stride=t_rows), :] = value

    def get(t_rows, g):
        return flat[pl.ds(g, 64, stride=t_rows), :]

    def pack(t_rows, dst):
        dst[...] = flat[0 : 64 * t_rows, :].astype(bf16).reshape(dst.shape)

    def unpack(t_rows, src):
        flat[0 : 64 * t_rows, :] = src[...].reshape(64 * t_rows, LANES).astype(f32)

    def grid_of(t_rows, first):
        tiles = [None] * 24
        for gg in range(3):
            x = jnp.concatenate([get(t_rows, first + 3 * gg + q) for q in range(3)], axis=1)
            x = block_transpose(x)
            for r in range(8):
                tiles[r * 3 + gg] = x[8 * r : 8 * r + 8]
        return jnp.concatenate(tiles, axis=0)

    def put_grid(t_rows, first, grid):
        for gg in range(3):
            x = jnp.concatenate([grid[8 * (3 * r + gg) : 8 * (3 * r + gg) + 8] for r in range(8)], axis=0)
            x = block_transpose(x)
            for q in range(3):
                put(t_rows, first + 3 * gg + q, x[:, LANES * q : LANES * q + LANES])

    def chunk(g):
        return pl.ds(g * LANES, LANES)

    w_four = jnp.concatenate([wga_ref[...], wpa_ref[...], wgb_ref[...], wpb_ref[...]], axis=0)
    for g in range(CHUNKS):
        values = pair_ref[chunk(g), :].astype(f32)
        centred = values - jnp.mean(values, -1, keepdims=True)
        spread = jnp.mean(centred * centred, -1, keepdims=True)
        inverse = lax.rsqrt(spread + epsilon)
        hat_g = centred * inverse
        hat[chunk(g), :] = hat_g
        rstd1[chunk(g), :] = inverse
        normed_g = hat_g.astype(bf16)
        normed[chunk(g), :] = normed_g
        projected = nt(w_four, normed_g)
        gate_a = sigmoid(projected[0:64])
        proj_a = projected[64:128]
        gate_b = sigmoid(projected[128:192])
        proj_b = projected[192:256]
        acts[g, 0:64, :] = gate_a
        acts[g, 64:128, :] = proj_a
        acts[g, 128:192, :] = gate_b
        acts[g, 192:256, :] = proj_b
        put(18, g, gate_a * proj_a)
        put(18, 9 + g, gate_b * proj_b)
    pack(18, send1)

    @pl.when(own)
    def _():
        pl.semaphore_wait(barrier, 64)

    @pl.when(jnp.logical_not(own))
    def _():
        pl.semaphore_wait(barrier, 65)

    swap_start(0, send1, recv1)

    copies = [partner(0, wgo_ref, wgo_other), partner(1, wo_ref, wo_other)]
    for copy in copies:
        copy.start()
    for g in range(CHUNKS):
        cot_t[:, chunk(g)] = jnp.transpose(cot_ref[chunk(g), :].astype(f32)).astype(bf16)
    copies.append(partner(2, cot_t, cot_other))
    copies[2].start()
    for copy in copies:
        copy.wait_recv()
    wgo = jnp.concatenate([wgo_ref[...], wgo_other[...]], axis=0)
    for g in range(CHUNKS):
        gate_out[:, chunk(g)] = sigmoid(nt(wgo, normed[chunk(g), :]))
    mine_rows = pl.ds(pl.multiple_of(ch * 64, 64), 64)
    wo_cols = jnp.concatenate([wo_ref[...], wo_other[...]], axis=0).astype(f32)
    wo_t = jnp.where(ch == 0, wo_cols, pltpu.roll(wo_cols, 64, 1))
    wo = jnp.transpose(wo_t).astype(bf16)
    wo_t = wo_t.astype(bf16)

    swap_wait(0, recv1)
    unpack(18, recv1)
    mine_half = pl.ds(pl.multiple_of(ch * 192, 192), 192)
    other_half = pl.ds(pl.multiple_of((1 - ch) * 192, 192), 192)
    right[mine_half, :] = grid_of(18, 9).astype(bf16)
    right_copy = partner(3, right.at[mine_half, :], right.at[mine_half, :])
    right_copy.start()
    left[...] = grid_of(18, 0).astype(bf16)
    right_copy.wait_recv()
    put_grid(10, 0, nt(left[...], right[...]))
    pack(10, send2)
    swap_start(1, send2, recv2.at[0])
    swap_wait(1, recv2.at[0])
    mixed_copy = partner(4, recv2.at[0], recv2.at[1])
    mixed_copy.start()
    mixed_copy.wait_recv()

    flat_two = []
    unpack(10, recv2.at[0])
    first = [get(10, g) for g in range(CHUNKS)]
    for g in range(CHUNKS):
        mixn_f = first[g]
        dfour[0:64, chunk(g)] = mixn_f.astype(bf16)
    unpack(10, recv2.at[1])
    for g in range(CHUNKS):
        mixed = jnp.concatenate([dfour[0:64, chunk(g)].astype(f32), get(10, g)], axis=0)
        mean = jnp.mean(mixed, 0, keepdims=True)
        var = jnp.mean(mixed * mixed, 0, keepdims=True) - mean * mean
        inverse = lax.rsqrt(var + epsilon)
        mixed_hat = (mixed - mean) * inverse
        mixed_norm = mixed_hat.astype(bf16)
        mixn[:, chunk(g)] = mixed_norm
        gate = gate_out[:, chunk(g)]
        proj_out = nn(wo_t, mixed_norm)
        upstream = jnp.concatenate([cot_t[:, chunk(g)], cot_other[:, chunk(g)]], axis=0).astype(f32)
        d_proj = (upstream * gate).astype(bf16)
        d_norm = nn(wo, d_proj)
        d_mean = jnp.mean(d_norm, 0, keepdims=True)
        d_cross = jnp.mean(d_norm * mixed_hat, 0, keepdims=True)
        d_mixed = inverse[:, :] * (d_norm[0:64] - d_mean - mixed_hat[0:64] * d_cross)
        acts_flat = d_mixed
        dmix_rows = acts_flat
        flat_two.append(dmix_rows)
        dproj[:, chunk(g)] = d_proj[0:64]
        gate_mine, proj_mine = gate[0:64], proj_out[0:64]
        dgate[:, chunk(g)] = (upstream[0:64] * proj_mine * gate_mine * (1.0 - gate_mine)).astype(bf16)
        updated_ref[chunk(g), :] = jnp.transpose(gate_mine * proj_mine).astype(bf16)
    for g in range(CHUNKS):
        put(10, g, flat_two[g])
    pack(10, send3)
    swap_start(2, send3, recv3)
    head_gate = nn(dgate[...], normed[...])
    head_out = nt(dproj[...], mixn[...])

    swap_wait(2, recv3)
    unpack(10, recv3)
    d_grid = grid_of(10, 0).astype(bf16)
    d_right = tn(d_grid, left[...])
    dr_send[...] = d_right.astype(bf16)
    dr_copy = partner(5, dr_send.at[other_half, :], dr_recv)
    dr_copy.start()
    put_grid(18, 0, nn(d_grid, right[...]))
    dr_copy.wait_recv()
    put_grid(18, 9, dr_send[mine_half, :].astype(f32) + dr_recv[...].astype(f32))
    pack(18, send4)
    swap_start(3, send4, recv4)
    swap_wait(3, recv4)
    unpack(18, recv4)
    for g in range(CHUNKS):
        d_left, d_right_g = get(18, g), get(18, 9 + g)
        gate_a, proj_a = acts[g, 0:64, :], acts[g, 64:128, :]
        gate_b, proj_b = acts[g, 128:192, :], acts[g, 192:256, :]
        dfour[0:64, chunk(g)] = (d_left * proj_a * gate_a * (1.0 - gate_a)).astype(bf16)
        dfour[64:128, chunk(g)] = (d_left * gate_a).astype(bf16)
        dfour[128:192, chunk(g)] = (d_right_g * proj_b * gate_b * (1.0 - gate_b)).astype(bf16)
        dfour[192:256, chunk(g)] = (d_right_g * gate_b).astype(bf16)
    edge = nn(dfour[...], normed[...])

    for k in range(4):
        put(6, k, edge[64 * k : 64 * k + 64])
    put(6, 4, head_gate)
    put(6, 5, jnp.where(ch == 0, head_out, pltpu.roll(head_out, 64, 1)))
    pack(6, send5)
    swap_start(4, send5, recv5)
    for g in range(CHUNKS):
        d_flat = tn(dfour[:, chunk(g)], w_four) + tn(dgate[:, chunk(g)], wgo_ref[...])
        df_send[chunk(g), :] = d_flat.astype(bf16)
    df_copy = partner(6, df_send, df_recv)
    df_copy.start()
    swap_wait(4, recv5)
    unpack(6, recv5)
    part_send[...] = jnp.zeros_like(part_send)
    for k in range(6):
        part_send[k : k + 1, :] = jnp.sum(get(6, k), 0, keepdims=True)
    part_copy = partner(7, part_send, part_recv)
    part_copy.start()
    part_copy.wait_recv()
    send6[...] = (part_send[...] + part_recv[...])[0:6].astype(bf16).reshape(send6.shape)
    swap_start(5, send6, recv6, one=True)

    df_copy.wait_recv()
    for g in range(CHUNKS):
        grad_whole = df_send[chunk(g), :].astype(f32) + df_recv[chunk(g), :].astype(f32)
        hat_g = hat[chunk(g), :]
        grad_full = rstd1[chunk(g), :] * (
            grad_whole
            - jnp.mean(grad_whole, -1, keepdims=True)
            - hat_g * jnp.mean(grad_whole * hat_g, -1, keepdims=True)
        )
        grad_full = jnp.where(ch == 0, grad_full, pltpu.roll(grad_full, 64, 1))
        grad_ref[chunk(g), :] = grad_full[:, 0:64].astype(bf16)

    swap_wait(5, recv6)
    unpack(6, recv6)
    for k, g_ref in enumerate((g0_ref, g1_ref, g2_ref, g3_ref, g4_ref, g5_ref)):
        g_ref[...] = get(6, k) * (1.0 / 384)

    for n, dst in enumerate((recv1, recv2.at[0], recv3, recv4, recv5, recv6)):
        swap_drain(n, dst)
    for copy in copies + [right_copy, mixed_copy, dr_copy, df_copy, part_copy]:
        copy.wait_send()


def on_device(pair, cotangent, w_gate_a, w_proj_a, w_gate_b, w_proj_b, w_gate_out, w_out):
    rows, cols, channels = pair.shape
    whole = pl.BlockSpec(memory_space=pltpu.VMEM)
    weights = [w.T for w in (w_gate_a, w_proj_a, w_gate_b, w_proj_b, w_gate_out, w_out)]
    vm = pltpu.VMEM
    big, small, tiny = (64, 9, 2, 128), (64, 5, 2, 128), (64, 3, 2, 128)
    outs = pl.pallas_call(
        kernel,
        out_shape=[
            jax.ShapeDtypeStruct((PAIRS, 64), bf16),
            jax.ShapeDtypeStruct((PAIRS, 64), bf16),
        ]
        + [jax.ShapeDtypeStruct((64, 128), f32)] * 6,
        in_specs=[whole] * 8,
        out_specs=[whole] * 8,
        scratch_shapes=[
            vm((PAIRS, 128), bf16),
            vm((PAIRS, 128), f32),
            vm((PAIRS, 1), f32),
            vm((CHUNKS, 256, 128), f32),
            vm((PAIRS, 128), f32),
            vm(big, bf16), vm(big, bf16),
            vm(small, bf16), vm((2,) + small, bf16),
            vm(small, bf16), vm(small, bf16),
            vm(big, bf16), vm(big, bf16),
            vm(tiny, bf16), vm(tiny, bf16),
            vm((3, 2, 128), bf16), vm(tiny, bf16),
            vm((192, 384), bf16), vm((384, 384), bf16),
            vm((384, 384), bf16), vm((192, 384), bf16),
            vm((PAIRS, 128), bf16), vm((PAIRS, 128), bf16),
            vm((8, 128), f32), vm((8, 128), f32),
            vm((64, 128), bf16), vm((64, 128), bf16),
            vm((64, PAIRS), bf16), vm((64, PAIRS), bf16),
            vm((128, PAIRS), f32),
            vm((64, PAIRS), bf16), vm((64, PAIRS), bf16),
            vm((128, PAIRS), bf16),
            vm((256, PAIRS), bf16),
            pltpu.SemaphoreType.DMA((6,)),
            pltpu.SemaphoreType.DMA((6,)),
            pltpu.SemaphoreType.DMA((8,)),
            pltpu.SemaphoreType.DMA((8,)),
        ],
        compiler_params=pltpu.CompilerParams(
            collective_id=0, has_side_effects=True, vmem_limit_bytes=40 << 20
        ),
    )(pair.reshape(PAIRS, channels), cotangent.reshape(PAIRS, 64), *weights)
    updated, grad_pair, ga, pa, gb, pb, go, out = outs
    return (
        updated.reshape(rows, cols, 64),
        grad_pair.reshape(rows, cols, 64),
        ga.T,
        pa.T,
        gb.T,
        pb.T,
        go.T,
        out.T,
    )


def solution(mesh):
    wide = P("row", "col", "ch")
    narrow = P(None, "ch")
    return jax.shard_map(
        on_device,
        mesh=mesh,
        in_specs=(P("row", "col", None), wide) + (narrow,) * 6,
        out_specs=(wide, wide) + (narrow,) * 6,
        check_vma=False,
    )
```

profile of v0, /device:TPU:1, one launch (start us, length us, event | category | flops | bytes accessed | tf_op | source)
XLA Modules:
  0.0 89.7 jit_solution(9641239012036644485)
XLA Ops:
  0.6 0.0 copy-start
  0.6 1.0 %copy-done = bf16[24,48,128]{2,1,0:T(8,128)(2,1)S(1)} copy-done((bf16[24,48,128]{2,1,0:T(8,128)(2,1)S(1)}, bf16[24,48,128]{2,1,0:T(8,128)(2,1)}, u32[]{:S(2)}) %copy-start) | copy-done | bytes 294936
  1.6 0.0 copy-start.1
  1.6 1.0 %copy-done.1 = bf16[24,48,64]{2,1,0:T(8,128)(2,1)S(1)} copy-done((bf16[24,48,64]{2,1,0:T(8,128)(2,1)S(1)}, bf16[24,48,64]{2,1,0:T(8,128)(2,1)}, u32[]{:S(2)}) %copy-start.1) | copy-done | bytes 147480
  2.6 0.0 copy-start.2
  2.6 0.7 copy-done.2
  3.3 0.0 copy-start.3
  3.3 0.7 copy-done.3
  4.0 0.0 copy-start.4
  4.0 0.7 copy-done.4
  4.7 0.0 copy-start.5
  4.7 0.7 copy-done.5
  5.4 0.0 copy-start.6
  5.4 0.7 copy-done.6
  6.2 0.7 copy-done.7
  6.9 77.7 %shard_map.143 = (bf16[1152,64]{1,0:T(8,128)(2,1)S(1)}, bf16[1152,64]{1,0:T(8,128)(2,1)S(1)}, f32[64,128]{1,0:T(8,128)S(1)}, f32[64,128]{1,0:T(8,128)S(1)}, f32[...) custom-call(bf16[1152,128]{1,0:T(8,128)(2,1)S(1)} %bitcast.18, ...), custom_call_target="tpu_custom_call" | custom-call | tf_op jit(solution)/shard_map/pallas_call | solution.py:334
  84.6 0.7 copy.24
  85.3 0.7 copy.25
  86.0 0.6 copy.26
  86.6 0.6 copy.27
  87.3 0.6 copy.28
  87.9 0.6 copy.29
  88.5 0.6 copy.30
  89.1 0.6 copy.31
  (1 shorter events, 0.0 us)
Async XLA Ops:
  0.6 1.0 %copy-start = (bf16[24,48,128]{2,1,0:T(8,128)(2,1)S(1)}, bf16[24,48,128]{2,1,0:T(8,128)(2,1)}, u32[]{:S(2)}) copy-start(bf16[24,48,128]{2,1,0:T(8,128)(2,1)} %param.8) | copy-start | bytes 884740
  1.6 1.0 %copy-start.1 = (bf16[24,48,64]{2,1,0:T(8,128)(2,1)S(1)}, bf16[24,48,64]{2,1,0:T(8,128)(2,1)}, u32[]{:S(2)}) copy-start(bf16[24,48,64]{2,1,0:T(8,128)(2,1)} %param.9) | copy-start | bytes 442372
  2.6 0.7 copy-start.2
  3.3 0.7 copy-start.3
  4.0 0.7 copy-start.4
  4.7 0.7 copy-start.5
  5.4 0.7 copy-start.6
  6.2 0.7 copy-start.7
where the time goes:
time: 90.4 us; the launch traced here: 89.7 us
  Pallas kernels  77.7 us (86%)
  local copies, waits for them, and re-layouts  11.3 us (12%)
    pallas_call x1, Pallas kernels, on_device(): pl.pallas_call(kernel, out_shape=[jax.ShapeDtypeStruct((PAIRS, 64), bf16)...  77.7 us
    unnamed x24, local copies, waits for them, and re-layouts  11.3 us

commit v1 on v0

--- a/solution.py
+++ b/solution.py
@@ -42,15 +42,30 @@
 
 
 def kernel(
-    pair_ref, cot_ref, wga_ref, wpa_ref, wgb_ref, wpb_ref, wgo_ref, wo_ref,
+    pair_hbm, cot_hbm, wga_hbm, wpa_hbm, wgb_hbm, wpb_hbm, wgo_hbm, wo_hbm,
     updated_ref, grad_ref, g0_ref, g1_ref, g2_ref, g3_ref, g4_ref, g5_ref,
-    normed, hat, rstd1, acts, flat,
-    send1, recv1, send2, recv2, send3, recv3, send4, recv4, send5, recv5, send6, recv6,
-    left, right, dr_send, dr_recv, df_send, df_recv, part_send, part_recv,
+    pair_ref, cot_ref, weights, load_sem, normed, hat, rstd1, acts, flat,
+    send1, recv1, send2, recv2, send3, recv3, send4, recv4,
+    send5, recv5, sendz, recvz, send6, recv6,
+    left, right, dr_send, dr_recv, df_send, df_recv,
     wgo_other, wo_other, cot_t, cot_other, gate_out, dproj, dgate, mixn, dfour,
-    send_sem, recv_sem, psend_sem, precv_sem,
+    send_sem, recv_sem, psend_sem, precv_sem, gsend_sem, grecv_sem,
 ):
+    loads = [
+        pltpu.make_async_copy(src, weights.at[pl.ds(64 * n, 64), :], load_sem.at[n])
+        for n, src in enumerate((wga_hbm, wpa_hbm, wgb_hbm, wpb_hbm, wgo_hbm, wo_hbm))
+    ]
+    loads += [
+        pltpu.make_async_copy(pair_hbm.at[rows, :], pair_ref.at[rows, :], load_sem.at[6 + n])
+        for n, rows in enumerate(pl.ds(384 * k, 384) for k in range(3))
+    ]
+    loads.append(pltpu.make_async_copy(cot_hbm, cot_ref, load_sem.at[9]))
+    for load in loads:
+        load.start()
+    wgo_ref, wo_ref = weights.at[pl.ds(256, 64), :], weights.at[pl.ds(320, 64), :]
+
     row, col, ch = lax.axis_index("row"), lax.axis_index("col"), lax.axis_index("ch")
+    x, y, z = row // 4, col // 2, (col % 2) * 4 + row % 4
     slot = (row % 8) * 8 + col
     half = row // 8
     own = half == ch
@@ -62,52 +77,92 @@
     barrier = pltpu.get_barrier_semaphore()
     pl.semaphore_signal(barrier, inc=1, device_id=other, device_id_type=MESH)
 
-    @pl.loop(1, 64)
-    def _(k):
-        pl.semaphore_signal(barrier, inc=1, device_id=peer((slot + k) % 64), device_id_type=MESH)
+    def each_peer(act):
+        @pl.loop(0, 8)
+        def _(k):
+            away = (4 + (1 - 2 * (k % 2)) * ((k + 1) // 2)) % 8
+            z_to = (z + away) % 8
+            for dy in (2, 1, 3, 0):
+                for dx in (1, 0):
+                    t = ((x + dx) % 2) * 32 + (z_to % 4) * 8 + ((y + dy) % 4) * 2 + z_to // 4
+                    if dy == 0 and dx == 0:
+
+                        @pl.when(k < 7)
+                        def _():
+                            act(t)
+                    else:
+                        act(t)
+
+    plane = [(2, 2), (2, 1), (2, 3), (1, 2), (3, 2), (2, 0), (0, 2), (1, 1), (1, 3), (3, 1), (3, 3)]
+    plane += [(1, 0), (3, 0), (0, 1), (0, 3)]
+
+    def plane_peer(dx, dy):
+        x_to, y_to = (x + dx) % 4, (y + dy) % 4
+        return x_to * 4 + y_to, (x_to * 4 + row % 4, y_to * 2 + col % 2, ch)
+
+    def line_peer(dz):
+        z_to = (z + dz) % 8
+        return (x * 4 + z_to % 4, y * 2 + z_to // 4, ch)
+
+    def greet(device):
+        pl.semaphore_signal(barrier, inc=1, device_id=device, device_id_type=MESH)
+
+    each_peer(lambda t: greet(peer(t)))
 
     @pl.when(jnp.logical_not(own))
     def _():
-        pl.semaphore_signal(barrier, inc=1, device_id=peer(slot), device_id_type=MESH)
-
-    def swap_start(n, src, dst, one=False):
-        def at(t):
-            return src if one else src.at[t]
-
+        greet(peer(slot))
+
+    for dx, dy in plane:
+        greet(plane_peer(dx, dy)[1])
+    for dz in (4, 3, 5, 2, 6, 1, 7):
+        greet(line_peer(dz))
+
+    def swap_start(n, src, dst, part):
         def copy(t):
             return pltpu.make_async_remote_copy(
-                src_ref=at(t),
-                dst_ref=dst.at[slot],
+                src_ref=src.at[t, part],
+                dst_ref=dst.at[slot, part],
                 send_sem=send_sem.at[n],
                 recv_sem=recv_sem.at[n],
                 device_id=peer(t),
                 device_id_type=MESH,
             )
 
+        each_peer(lambda t: copy(t).start())
+
         @pl.when(own)
         def _():
-            pltpu.make_async_copy(at(slot), dst.at[slot], recv_sem.at[n]).start()
+            pltpu.make_async_copy(src.at[slot, part], dst.at[slot, part], recv_sem.at[n]).start()
 
         @pl.when(jnp.logical_not(own))
         def _():
             copy(slot).start()
 
-        @pl.loop(1, 64)
-        def _(k):
-            copy((slot + k) % 64).start()
-
-    def swap_wait(n, dst):
-        pltpu.make_async_copy(dst, dst, recv_sem.at[n]).wait()
-
-    def swap_drain(n, dst):
+    def swap_wait(n, dst, part):
+        whole = dst.at[:, part]
+        pltpu.make_async_copy(whole, whole, recv_sem.at[n]).wait()
+
+    def swap_drain(n, dst, part):
         @pl.when(own)
         def _():
-            some = dst.at[pl.ds(0, 63)]
+            some = dst.at[pl.ds(0, 63), part]
             pltpu.make_async_copy(some, some, send_sem.at[n]).wait()
 
         @pl.when(jnp.logical_not(own))
         def _():
-            pltpu.make_async_copy(dst, dst, send_sem.at[n]).wait()
+            whole = dst.at[:, part]
+            pltpu.make_async_copy(whole, whole, send_sem.at[n]).wait()
+
+    def group_copy(n, src, dst, device):
+        return pltpu.make_async_remote_copy(
+            src_ref=src,
+            dst_ref=dst,
+            send_sem=gsend_sem.at[n],
+            recv_sem=grecv_sem.at[n],
+            device_id=device,
+            device_id_type=MESH,
+        )
 
     def partner(n, src, dst):
         return pltpu.make_async_remote_copy(
@@ -128,6 +183,9 @@
     def pack(t_rows, dst):
         dst[...] = flat[0 : 64 * t_rows, :].astype(bf16).reshape(dst.shape)
 
+    ten, early, late = pl.ds(0, 5), pl.ds(0, 5), pl.ds(5, 4)
+    head, tail = pl.ds(0, 4), pl.ds(4, 5)
+
     def unpack(t_rows, src):
         flat[0 : 64 * t_rows, :] = src[...].reshape(64 * t_rows, LANES).astype(f32)
 
@@ -150,8 +208,12 @@
     def chunk(g):
         return pl.ds(g * LANES, LANES)
 
-    w_four = jnp.concatenate([wga_ref[...], wpa_ref[...], wgb_ref[...], wpb_ref[...]], axis=0)
-    for g in range(CHUNKS):
+    for load in loads[0:6]:
+        load.wait()
+    w_four = weights[0:256, :]
+    for g in range(CHUNKS):
+        if g % 3 == 0:
+            loads[6 + g // 3].wait()
         values = pair_ref[chunk(g), :].astype(f32)
         centred = values - jnp.mean(values, -1, keepdims=True)
         spread = jnp.mean(centred * centred, -1, keepdims=True)
@@ -170,23 +232,25 @@
         acts[g, 64:128, :] = proj_a
         acts[g, 128:192, :] = gate_b
         acts[g, 192:256, :] = proj_b
-        put(18, g, gate_a * proj_a)
-        put(18, 9 + g, gate_b * proj_b)
+        put(18, g, gate_b * proj_b)
+        put(18, 9 + g, gate_a * proj_a)
     pack(18, send1)
 
     @pl.when(own)
     def _():
-        pl.semaphore_wait(barrier, 64)
+        pl.semaphore_wait(barrier, 86)
 
     @pl.when(jnp.logical_not(own))
     def _():
-        pl.semaphore_wait(barrier, 65)
-
-    swap_start(0, send1, recv1)
+        pl.semaphore_wait(barrier, 87)
+
+    swap_start(0, send1, recv1, early)
+    swap_start(1, send1, recv1, late)
 
     copies = [partner(0, wgo_ref, wgo_other), partner(1, wo_ref, wo_other)]
     for copy in copies:
         copy.start()
+    loads[9].wait()
     for g in range(CHUNKS):
         cot_t[:, chunk(g)] = jnp.transpose(cot_ref[chunk(g), :].astype(f32)).astype(bf16)
     copies.append(partner(2, cot_t, cot_other))
@@ -202,19 +266,21 @@
     wo = jnp.transpose(wo_t).astype(bf16)
     wo_t = wo_t.astype(bf16)
 
-    swap_wait(0, recv1)
-    unpack(18, recv1)
+    swap_wait(0, recv1, early)
     mine_half = pl.ds(pl.multiple_of(ch * 192, 192), 192)
     other_half = pl.ds(pl.multiple_of((1 - ch) * 192, 192), 192)
-    right[mine_half, :] = grid_of(18, 9).astype(bf16)
+    flat[0:640, :] = recv1[:, early].reshape(640, LANES).astype(f32)
+    right[mine_half, :] = grid_of(10, 0).astype(bf16)
     right_copy = partner(3, right.at[mine_half, :], right.at[mine_half, :])
     right_copy.start()
-    left[...] = grid_of(18, 0).astype(bf16)
+    swap_wait(1, recv1, late)
+    unpack(18, recv1)
+    left[...] = grid_of(18, 9).astype(bf16)
     right_copy.wait_recv()
     put_grid(10, 0, nt(left[...], right[...]))
     pack(10, send2)
-    swap_start(1, send2, recv2.at[0])
-    swap_wait(1, recv2.at[0])
+    swap_start(2, send2, recv2.at[0], ten)
+    swap_wait(2, recv2.at[0], ten)
     mixed_copy = partner(4, recv2.at[0], recv2.at[1])
     mixed_copy.start()
     mixed_copy.wait_recv()
@@ -252,11 +318,11 @@
     for g in range(CHUNKS):
         put(10, g, flat_two[g])
     pack(10, send3)
-    swap_start(2, send3, recv3)
+    swap_start(3, send3, recv3, ten)
     head_gate = nn(dgate[...], normed[...])
     head_out = nt(dproj[...], mixn[...])
 
-    swap_wait(2, recv3)
+    swap_wait(3, recv3, ten)
     unpack(10, recv3)
     d_grid = grid_of(10, 0).astype(bf16)
     d_right = tn(d_grid, left[...])
@@ -264,11 +330,14 @@
     dr_copy = partner(5, dr_send.at[other_half, :], dr_recv)
     dr_copy.start()
     put_grid(18, 0, nn(d_grid, right[...]))
+    send4[:, head] = flat[...].astype(bf16).reshape(send4.shape)[:, 0:4]
+    swap_start(4, send4, recv4, head)
     dr_copy.wait_recv()
     put_grid(18, 9, dr_send[mine_half, :].astype(f32) + dr_recv[...].astype(f32))
-    pack(18, send4)
-    swap_start(3, send4, recv4)
-    swap_wait(3, recv4)
+    send4[:, tail] = flat[...].astype(bf16).reshape(send4.shape)[:, 4:9]
+    swap_start(5, send4, recv4, tail)
+    swap_wait(4, recv4, head)
+    swap_wait(5, recv4, tail)
     unpack(18, recv4)
     for g in range(CHUNKS):
         d_left, d_right_g = get(18, g), get(18, 9 + g)
@@ -285,23 +354,21 @@
     put(6, 4, head_gate)
     put(6, 5, jnp.where(ch == 0, head_out, pltpu.roll(head_out, 64, 1)))
     pack(6, send5)
-    swap_start(4, send5, recv5)
+    e_me, _ = plane_peer(0, 0)
+    for dx, dy in plane:
+        e, device = plane_peer(dx, dy)
+        group_copy(0, send5.at[e], recv5.at[e_me], device).start()
+    pltpu.make_async_copy(send5.at[e_me], recv5.at[e_me], grecv_sem.at[0]).start()
     for g in range(CHUNKS):
         d_flat = tn(dfour[:, chunk(g)], w_four) + tn(dgate[:, chunk(g)], wgo_ref[...])
         df_send[chunk(g), :] = d_flat.astype(bf16)
     df_copy = partner(6, df_send, df_recv)
     df_copy.start()
-    swap_wait(4, recv5)
-    unpack(6, recv5)
-    part_send[...] = jnp.zeros_like(part_send)
-    for k in range(6):
-        part_send[k : k + 1, :] = jnp.sum(get(6, k), 0, keepdims=True)
-    part_copy = partner(7, part_send, part_recv)
-    part_copy.start()
-    part_copy.wait_recv()
-    send6[...] = (part_send[...] + part_recv[...])[0:6].astype(bf16).reshape(send6.shape)
-    swap_start(5, send6, recv6, one=True)
-
+    pltpu.make_async_copy(recv5, recv5, grecv_sem.at[0]).wait()
+    sendz[...] = jnp.sum(recv5[...].astype(f32), 0).astype(bf16)
+    for dz in (4, 3, 5, 2, 6, 1, 7):
+        group_copy(1, sendz, recvz.at[z], line_peer(dz)).start()
+    pltpu.make_async_copy(sendz, recvz.at[z], grecv_sem.at[1]).start()
     df_copy.wait_recv()
     for g in range(CHUNKS):
         grad_whole = df_send[chunk(g), :].astype(f32) + df_recv[chunk(g), :].astype(f32)
@@ -314,15 +381,36 @@
         grad_full = jnp.where(ch == 0, grad_full, pltpu.roll(grad_full, 64, 1))
         grad_ref[chunk(g), :] = grad_full[:, 0:64].astype(bf16)
 
-    swap_wait(5, recv6)
-    unpack(6, recv6)
+    pltpu.make_async_copy(recvz, recvz, grecv_sem.at[1]).wait()
+    send6[...] = jnp.sum(recvz[...].astype(f32), 0).astype(bf16)
+    for dx, dy in plane:
+        _, device = plane_peer(dx, dy)
+        group_copy(2, send6, recv6.at[e_me], device).start()
+    pltpu.make_async_copy(send6, recv6.at[e_me], grecv_sem.at[2]).start()
+    pltpu.make_async_copy(recv6, recv6, grecv_sem.at[2]).wait()
+    flat[0:384, :] = recv6[...].reshape(384, LANES).astype(f32)
     for k, g_ref in enumerate((g0_ref, g1_ref, g2_ref, g3_ref, g4_ref, g5_ref)):
         g_ref[...] = get(6, k) * (1.0 / 384)
 
-    for n, dst in enumerate((recv1, recv2.at[0], recv3, recv4, recv5, recv6)):
-        swap_drain(n, dst)
-    for copy in copies + [right_copy, mixed_copy, dr_copy, df_copy, part_copy]:
+    swap_drain(0, recv1, early)
+    swap_drain(1, recv1, late)
+    swap_drain(2, recv2.at[0], ten)
+    swap_drain(3, recv3, ten)
+    swap_drain(4, recv4, head)
+    swap_drain(5, recv4, tail)
+    pltpu.make_async_copy(recv5.at[pl.ds(0, 15)], recv5.at[pl.ds(0, 15)], gsend_sem.at[0]).wait()
+    pltpu.make_async_copy(recvz.at[pl.ds(0, 7)], recvz.at[pl.ds(0, 7)], gsend_sem.at[1]).wait()
+    pltpu.make_async_copy(recv6.at[pl.ds(0, 15)], recv6.at[pl.ds(0, 15)], gsend_sem.at[2]).wait()
+    for copy in copies + [right_copy, mixed_copy, dr_copy, df_copy]:
         copy.wait_send()
+
+
+def write_kernel(*refs):
+    copies = [pltpu.make_async_copy(refs[n], refs[8 + n], refs[16].at[n]) for n in range(8)]
+    for copy in copies:
+        copy.start()
+    for copy in copies:
+        copy.wait()
 
 
 def on_device(pair, cotangent, w_gate_a, w_proj_a, w_gate_b, w_proj_b, w_gate_out, w_out):
@@ -330,17 +418,17 @@
     whole = pl.BlockSpec(memory_space=pltpu.VMEM)
     weights = [w.T for w in (w_gate_a, w_proj_a, w_gate_b, w_proj_b, w_gate_out, w_out)]
     vm = pltpu.VMEM
-    big, small, tiny = (64, 9, 2, 128), (64, 5, 2, 128), (64, 3, 2, 128)
+    big, small = (64, 9, 2, 128), (64, 5, 2, 128)
+    sixteen, eight, one = (16, 24, 128), (8, 24, 128), (24, 128)
+    shapes = [jax.ShapeDtypeStruct((PAIRS, 64), bf16)] * 2 + [jax.ShapeDtypeStruct((64, 128), f32)] * 6
     outs = pl.pallas_call(
         kernel,
-        out_shape=[
-            jax.ShapeDtypeStruct((PAIRS, 64), bf16),
-            jax.ShapeDtypeStruct((PAIRS, 64), bf16),
-        ]
-        + [jax.ShapeDtypeStruct((64, 128), f32)] * 6,
-        in_specs=[whole] * 8,
+        out_shape=shapes,
+        in_specs=[pl.BlockSpec(memory_space=pl.ANY)] * 8,
         out_specs=[whole] * 8,
         scratch_shapes=[
+            vm((PAIRS, 128), bf16), vm((PAIRS, 64), bf16), vm((384, 128), bf16),
+            pltpu.SemaphoreType.DMA((10,)),
             vm((PAIRS, 128), bf16),
             vm((PAIRS, 128), f32),
             vm((PAIRS, 1), f32),
@@ -350,12 +438,12 @@
             vm(small, bf16), vm((2,) + small, bf16),
             vm(small, bf16), vm(small, bf16),
             vm(big, bf16), vm(big, bf16),
-            vm(tiny, bf16), vm(tiny, bf16),
-            vm((3, 2, 128), bf16), vm(tiny, bf16),
+            vm(sixteen, bf16), vm(sixteen, bf16),
+            vm(one, bf16), vm(eight, bf16),
+            vm(one, bf16), vm(sixteen, bf16),
             vm((192, 384), bf16), vm((384, 384), bf16),
             vm((384, 384), bf16), vm((192, 384), bf16),
             vm((PAIRS, 128), bf16), vm((PAIRS, 128), bf16),
-            vm((8, 128), f32), vm((8, 128), f32),
             vm((64, 128), bf16), vm((64, 128), bf16),
             vm((64, PAIRS), bf16), vm((64, PAIRS), bf16),
             vm((128, PAIRS), f32),
@@ -366,11 +454,20 @@
             pltpu.SemaphoreType.DMA((6,)),
             pltpu.SemaphoreType.DMA((8,)),
             pltpu.SemaphoreType.DMA((8,)),
+            pltpu.SemaphoreType.DMA((3,)),
+            pltpu.SemaphoreType.DMA((3,)),
         ],
         compiler_params=pltpu.CompilerParams(
             collective_id=0, has_side_effects=True, vmem_limit_bytes=40 << 20
         ),
     )(pair.reshape(PAIRS, channels), cotangent.reshape(PAIRS, 64), *weights)
+    outs = pl.pallas_call(
+        write_kernel,
+        out_shape=shapes,
+        in_specs=[whole] * 8,
+        out_specs=[pl.BlockSpec(memory_space=pl.ANY)] * 8,
+        scratch_shapes=[pltpu.SemaphoreType.DMA((8,))],
+    )(*outs)
     updated, grad_pair, ga, pa, gb, pb, go, out = outs
     return (
         updated.reshape(rows, cols, 64),

time: 90.4 us -> 82 us (0.907)
  Pallas kernels: 77.7 us -> 69.4 us
    pallas_call x1 -> x2, Pallas kernels: 77.7 us -> 69.4 us  [the longest x1 67.4 us: on_device(): pl.pallas_call(kernel, out_shape=shapes, in_specs=[pl.BlockSpec(memory_sp...]
    unnamed x24 -> x32, local copies, waits for them, and re-layouts: 11.3 us -> 11.2 us
where the time goes in v1:
time: 82 us; the launch traced here: 81.4 us
  Pallas kernels  69.4 us (85%)
  local copies, waits for them, and re-layouts  11.2 us (14%)
    pallas_call x1, Pallas kernels, on_device(): pl.pallas_call(kernel, out_shape=shapes, in_specs=[pl.BlockSpec(memory_sp...  67.4 us
    unnamed x32, local copies, waits for them, and re-layouts  11.2 us
    pallas_call x1, Pallas kernels, on_device(): pl.pallas_call(write_kernel, out_shape=shapes, in_specs=[whole] * 8, out_...  2.03 us

profile of v1, /device:TPU:1, one launch (start us, length us, event | category | flops | bytes accessed | tf_op | source)
XLA Modules:
  0.0 81.4 jit_solution(135960677223414747)
XLA Ops:
  0.6 0.0 copy-start.2
  0.6 1.0 %copy-done.2 = bf16[24,48,128]{2,1,0:T(8,128)(2,1)S(1)} copy-done((bf16[24,48,128]{2,1,0:T(8,128)(2,1)S(1)}, bf16[24,48,128]{2,1,0:T(8,128)(2,1)}, u32[]{:S(2)}) %copy-start.2) | copy-done | bytes 294936
  1.6 0.0 copy-start.3
  1.6 1.0 %copy-done.3 = bf16[24,48,64]{2,1,0:T(8,128)(2,1)S(1)} copy-done((bf16[24,48,64]{2,1,0:T(8,128)(2,1)S(1)}, bf16[24,48,64]{2,1,0:T(8,128)(2,1)}, u32[]{:S(2)}) %copy-start.3) | copy-done | bytes 147480
  2.6 0.0 copy-start.10
  2.6 0.7 copy-done.10
  3.3 0.0 copy-start.11
  3.3 0.7 copy-done.11
  4.0 0.0 copy-start.12
  4.0 0.7 copy-done.12
  4.7 0.7 copy-done.13
  5.4 0.7 copy-done.14
  6.2 0.7 copy-done.15
  6.9 67.4 %shard_map.143 = (bf16[1152,64]{1,0:T(8,128)(2,1)S(1)}, bf16[1152,64]{1,0:T(8,128)(2,1)S(1)}, f32[64,128]{1,0:T(8,128)S(1)}, f32[64,128]{1,0:T(8,128)S(1)}, f32[...) custom-call(bf16[1152,128]{1,0:T(8,128)(2,1)S(1)} %bitcast.16, ...), custom_call_target="tpu_custom_call" | custom-call | tf_op jit(solution)/shard_map/pallas_call | solution.py:424
  74.3 0.0 copy-start
  74.3 0.7 copy-done
  75.0 0.7 copy-done.1
  75.7 0.6 copy-done.4
  76.3 0.6 copy-done.5
  76.9 0.6 copy-done.6
  77.5 0.6 copy-done.7
  78.1 0.6 copy-done.8
  78.7 0.6 copy-done.9
  79.3 2.0 %shard_map.144 = (bf16[1152,64]{1,0:T(8,128)(2,1)}, bf16[1152,64]{1,0:T(8,128)(2,1)}, f32[64,128]{1,0:T(8,128)}, f32[64,128]{1,0:T(8,128)}, f32[64,128]{1,0:T(8,...) custom-call(bf16[1152,64]{1,0:T(8,128)(2,1)} %copy-done, bf16[1152,64]{1,0:T(8,128)(2,1)} %copy-done.1, ...), custom_call_target="tpu_custom_call" | custom-call | tf_op jit(solution)/shard_map/pallas_call | solution.py:464
  (10 shorter events, 0.0 us)
Async XLA Ops:
  0.6 1.0 %copy-start.2 = (bf16[24,48,128]{2,1,0:T(8,128)(2,1)S(1)}, bf16[24,48,128]{2,1,0:T(8,128)(2,1)}, u32[]{:S(2)}) copy-start(bf16[24,48,128]{2,1,0:T(8,128)(2,1)} %param.8) | copy-start | bytes 884740
  1.6 1.0 %copy-start.3 = (bf16[24,48,64]{2,1,0:T(8,128)(2,1)S(1)}, bf16[24,48,64]{2,1,0:T(8,128)(2,1)}, u32[]{:S(2)}) copy-start(bf16[24,48,64]{2,1,0:T(8,128)(2,1)} %param.9) | copy-start | bytes 442372
  2.6 0.7 copy-start.10
  3.3 0.7 copy-start.11
  4.0 0.7 copy-start.12
  4.7 0.7 copy-start.13
  5.4 0.7 copy-start.14
  6.2 0.7 copy-start.15
  74.3 0.7 copy-start
  75.0 0.7 copy-start.1
  75.7 0.6 copy-start.4
  76.3 0.6 copy-start.5
  76.9 0.6 copy-start.6
  77.5 0.6 copy-start.7
  78.1 0.6 copy-start.8
  78.7 0.6 copy-start.9

commit v2 on v1

--- a/solution.py
+++ b/solution.py
@@ -424,7 +424,7 @@
     outs = pl.pallas_call(
         kernel,
         out_shape=shapes,
-        in_specs=[pl.BlockSpec(memory_space=pl.ANY)] * 8,
+        in_specs=[pl.BlockSpec(memory_space=pltpu.HBM)] * 8,
         out_specs=[whole] * 8,
         scratch_shapes=[
             vm((PAIRS, 128), bf16), vm((PAIRS, 64), bf16), vm((384, 128), bf16),
@@ -460,13 +460,14 @@
         compiler_params=pltpu.CompilerParams(
             collective_id=0, has_side_effects=True, vmem_limit_bytes=40 << 20
         ),
-    )(pair.reshape(PAIRS, channels), cotangent.reshape(PAIRS, 64), *weights)
+    )(*[pltpu.with_memory_space_constraint(a, pltpu.HBM) for a in (pair.reshape(PAIRS, channels), cotangent.reshape(PAIRS, 64), *weights)])
     outs = pl.pallas_call(
         write_kernel,
         out_shape=shapes,
         in_specs=[whole] * 8,
-        out_specs=[pl.BlockSpec(memory_space=pl.ANY)] * 8,
+        out_specs=[pl.BlockSpec(memory_space=pltpu.HBM)] * 8,
         scratch_shapes=[pltpu.SemaphoreType.DMA((8,))],
+        compiler_params=pltpu.CompilerParams(vmem_limit_bytes=4 << 20),
     )(*outs)
     updated, grad_pair, ga, pa, gb, pb, go, out = outs
     return (

time: 82 us -> 68.4 us (0.83)
  local copies, waits for them, and re-layouts: 11.2 us -> 0 us
  Pallas kernels: 69.4 us -> 67.7 us
    unnamed x32 -> x0, local copies, waits for them, and re-layouts: 11.2 us -> none
    pallas_call x1, Pallas kernels: 2.03 us -> 0.94 us  [on_device(): pl.pallas_call(write_kernel, out_shape=shapes, in_specs=[whole] * 8, out_...]
where the time goes in v2:
time: 68.4 us; the launch traced here: 68.3 us
  Pallas kernels  67.7 us (99%)
    pallas_call x1, Pallas kernels, on_device(): pl.pallas_call(kernel, out_shape=shapes, in_specs=[pl.BlockSpec(memory_sp...  66.7 us

profile of v2, /device:TPU:1, one launch (start us, length us, event | category | flops | bytes accessed | tf_op | source)
XLA Modules:
  0.0 68.3 jit_solution(74636235425226595)
XLA Ops:
  0.6 66.7 %shard_map.143 = (bf16[1152,64]{1,0:T(8,128)(2,1)S(1)}, bf16[1152,64]{1,0:T(8,128)(2,1)S(1)}, f32[64,128]{1,0:T(8,128)S(1)}, f32[64,128]{1,0:T(8,128)S(1)}, f32[...) custom-call(bf16[1152,128]{1,0:T(8,128)(2,1)} %bitcast.16, ...), custom_call_target="tpu_custom_call" | custom-call | tf_op jit(solution)/shard_map/pallas_call | solution.py:424
  67.4 0.9 %shard_map.144 = (bf16[1152,64]{1,0:T(8,128)(2,1)}, bf16[1152,64]{1,0:T(8,128)(2,1)}, f32[64,128]{1,0:T(8,128)}, f32[64,128]{1,0:T(8,128)}, f32[64,128]{1,0:T(8,...) custom-call(bf16[1152,64]{1,0:T(8,128)(2,1)S(1)} %get-tuple-element.24.refs_0_, ...), custom_call_target="tpu_custom_call" | custom-call | tf_op jit(solution)/shard_map/pallas_call | solution.py:464

commit v3 on v2

--- a/solution.py
+++ b/solution.py
@@ -5,7 +5,7 @@
 from jax.experimental.pallas import tpu as pltpu
 from jax.sharding import PartitionSpec as P
 
-MESH = pl.DeviceIdType.MESH
+LOGICAL = pl.DeviceIdType.LOGICAL
 epsilon = 1e-05
 f32, bf16 = jnp.float32, jnp.bfloat16
 PAIRS, CHUNKS, LANES = 1152, 9, 128
@@ -25,6 +25,16 @@
 
 def sigmoid(x):
     return 1.0 / (1.0 + jnp.exp(-x))
+
+
+def hops(d):
+    return min(d[0], 8 - d[0]) + min(d[1], 4 - d[1]) + d[2]
+
+
+FAR_FIRST = sorted(
+    [(dz, dy, dx) for dz in range(8) for dy in range(4) for dx in range(2) if dz + dy + dx],
+    key=lambda d: -hops(d),
+)
 
 
 def block_transpose(x):
@@ -44,11 +54,11 @@
 def kernel(
     pair_hbm, cot_hbm, wga_hbm, wpa_hbm, wgb_hbm, wpb_hbm, wgo_hbm, wo_hbm,
     updated_ref, grad_ref, g0_ref, g1_ref, g2_ref, g3_ref, g4_ref, g5_ref,
-    pair_ref, cot_ref, weights, load_sem, normed, hat, rstd1, acts, flat,
-    send1, recv1, send2, recv2, send3, recv3, send4, recv4,
+    pair_ref, cot_ref, weights, load_sem, normed, hat, rstd1, acts, flat_a, flat_b, flat_c,
+    send1a, recv1a, send1b, recv1b, send2, recv2, send3, recv3, send4a, recv4a, send4b, recv4b,
     send5, recv5, sendz, recvz, send6, recv6,
-    left, right, dr_send, dr_recv, df_send, df_recv,
-    wgo_other, wo_other, cot_t, cot_other, gate_out, dproj, dgate, mixn, dfour,
+    left, right, dgrid_t, dr_send, dr_recv, df_send, df_recv,
+    wgo_other, wo_other, cot_t, cot_other, gate_out, proj_mine, dproj, dgate, mixn, dfour,
     send_sem, recv_sem, psend_sem, precv_sem, gsend_sem, grecv_sem,
 ):
     loads = [
@@ -69,43 +79,36 @@
     slot = (row % 8) * 8 + col
     half = row // 8
     own = half == ch
-    other = (row, col, 1 - ch)
+    other = row * 16 + col * 2 + 1 - ch
+
+    slot_z = [((z + dz) % 8 % 4) * 8 + (z + dz) % 8 // 4 for dz in range(8)]
+    slot_y = [((y + dy) % 4) * 2 for dy in range(4)]
+    slot_x = [((x + dx) % 2) * 32 for dx in range(2)]
+    base = 128 * ch + half
 
     def peer(t):
-        return (8 * ch + t // 8, t % 8, half)
+        return base + 2 * t
 
     barrier = pltpu.get_barrier_semaphore()
-    pl.semaphore_signal(barrier, inc=1, device_id=other, device_id_type=MESH)
+    pl.semaphore_signal(barrier, inc=1, device_id=other, device_id_type=LOGICAL)
 
     def each_peer(act):
-        @pl.loop(0, 8)
-        def _(k):
-            away = (4 + (1 - 2 * (k % 2)) * ((k + 1) // 2)) % 8
-            z_to = (z + away) % 8
-            for dy in (2, 1, 3, 0):
-                for dx in (1, 0):
-                    t = ((x + dx) % 2) * 32 + (z_to % 4) * 8 + ((y + dy) % 4) * 2 + z_to // 4
-                    if dy == 0 and dx == 0:
-
-                        @pl.when(k < 7)
-                        def _():
-                            act(t)
-                    else:
-                        act(t)
+        for dz, dy, dx in FAR_FIRST:
+            act(slot_z[dz] + slot_y[dy] + slot_x[dx])
 
     plane = [(2, 2), (2, 1), (2, 3), (1, 2), (3, 2), (2, 0), (0, 2), (1, 1), (1, 3), (3, 1), (3, 3)]
     plane += [(1, 0), (3, 0), (0, 1), (0, 3)]
 
     def plane_peer(dx, dy):
         x_to, y_to = (x + dx) % 4, (y + dy) % 4
-        return x_to * 4 + y_to, (x_to * 4 + row % 4, y_to * 2 + col % 2, ch)
+        return x_to * 4 + y_to, (x_to * 4 + row % 4) * 16 + (y_to * 2 + col % 2) * 2 + ch
 
     def line_peer(dz):
         z_to = (z + dz) % 8
-        return (x * 4 + z_to % 4, y * 2 + z_to // 4, ch)
+        return (x * 4 + z_to % 4) * 16 + (y * 2 + z_to // 4) * 2 + ch
 
     def greet(device):
-        pl.semaphore_signal(barrier, inc=1, device_id=device, device_id_type=MESH)
+        pl.semaphore_signal(barrier, inc=1, device_id=device, device_id_type=LOGICAL)
 
     each_peer(lambda t: greet(peer(t)))
 
@@ -118,41 +121,39 @@
     for dz in (4, 3, 5, 2, 6, 1, 7):
         greet(line_peer(dz))
 
-    def swap_start(n, src, dst, part):
+    def swap_start(n, src, dst):
         def copy(t):
             return pltpu.make_async_remote_copy(
-                src_ref=src.at[t, part],
-                dst_ref=dst.at[slot, part],
+                src_ref=src.at[t],
+                dst_ref=dst.at[slot],
                 send_sem=send_sem.at[n],
                 recv_sem=recv_sem.at[n],
                 device_id=peer(t),
-                device_id_type=MESH,
+                device_id_type=LOGICAL,
             )
 
         each_peer(lambda t: copy(t).start())
 
         @pl.when(own)
         def _():
-            pltpu.make_async_copy(src.at[slot, part], dst.at[slot, part], recv_sem.at[n]).start()
+            pltpu.make_async_copy(src.at[slot], dst.at[slot], recv_sem.at[n]).start()
 
         @pl.when(jnp.logical_not(own))
         def _():
             copy(slot).start()
 
-    def swap_wait(n, dst, part):
-        whole = dst.at[:, part]
-        pltpu.make_async_copy(whole, whole, recv_sem.at[n]).wait()
-
-    def swap_drain(n, dst, part):
+    def swap_wait(n, dst):
+        pltpu.make_async_copy(dst, dst, recv_sem.at[n]).wait()
+
+    def swap_drain(n, dst):
         @pl.when(own)
         def _():
-            some = dst.at[pl.ds(0, 63), part]
+            some = dst.at[pl.ds(0, 63)]
             pltpu.make_async_copy(some, some, send_sem.at[n]).wait()
 
         @pl.when(jnp.logical_not(own))
         def _():
-            whole = dst.at[:, part]
-            pltpu.make_async_copy(whole, whole, send_sem.at[n]).wait()
+            pltpu.make_async_copy(dst, dst, send_sem.at[n]).wait()
 
     def group_copy(n, src, dst, device):
         return pltpu.make_async_remote_copy(
@@ -161,7 +162,7 @@
             send_sem=gsend_sem.at[n],
             recv_sem=grecv_sem.at[n],
             device_id=device,
-            device_id_type=MESH,
+            device_id_type=LOGICAL,
         )
 
     def partner(n, src, dst):
@@ -171,39 +172,45 @@
             send_sem=psend_sem.at[n],
             recv_sem=precv_sem.at[n],
             device_id=other,
-            device_id_type=MESH,
+            device_id_type=LOGICAL,
         )
 
-    def put(t_rows, g, value):
-        flat[pl.ds(g, 64, stride=t_rows), :] = value
-
-    def get(t_rows, g):
-        return flat[pl.ds(g, 64, stride=t_rows), :]
-
-    def pack(t_rows, dst):
-        dst[...] = flat[0 : 64 * t_rows, :].astype(bf16).reshape(dst.shape)
-
-    ten, early, late = pl.ds(0, 5), pl.ds(0, 5), pl.ds(5, 4)
-    head, tail = pl.ds(0, 4), pl.ds(4, 5)
-
-    def unpack(t_rows, src):
-        flat[0 : 64 * t_rows, :] = src[...].reshape(64 * t_rows, LANES).astype(f32)
-
-    def grid_of(t_rows, first):
+    def put(flat, rows, k, value):
+        flat[pl.ds(k, 64, stride=rows), :] = value
+
+    def get(flat, rows, k):
+        return flat[pl.ds(k, 64, stride=rows), :]
+
+    def pack(flat, rows, dst):
+        dst[...] = flat[0 : 64 * rows, :].astype(bf16).reshape(dst.shape)
+
+    def unpack(flat, rows, src):
+        flat[0 : 64 * rows, :] = src[...].reshape(64 * rows, LANES).astype(f32)
+
+    def grid_of(row_of):
         tiles = [None] * 24
         for gg in range(3):
-            x = jnp.concatenate([get(t_rows, first + 3 * gg + q) for q in range(3)], axis=1)
+            x = jnp.concatenate([row_of(3 * gg + q) for q in range(3)], axis=1)
             x = block_transpose(x)
             for r in range(8):
                 tiles[r * 3 + gg] = x[8 * r : 8 * r + 8]
         return jnp.concatenate(tiles, axis=0)
 
-    def put_grid(t_rows, first, grid):
+    def put_grid(put_row, grid):
         for gg in range(3):
             x = jnp.concatenate([grid[8 * (3 * r + gg) : 8 * (3 * r + gg) + 8] for r in range(8)], axis=0)
             x = block_transpose(x)
             for q in range(3):
-                put(t_rows, first + 3 * gg + q, x[:, LANES * q : LANES * q + LANES])
+                put_row(3 * gg + q, x[:, LANES * q : LANES * q + LANES])
+
+    def put_left(k, value):
+        put(*((flat_a, 10, 9) if k == 0 else (flat_b, 8, k - 1)), value)
+
+    def get_left(k):
+        return get(flat_a, 10, 9) if k == 0 else get(flat_b, 8, k - 1)
+
+    def put_d_left(k, value):
+        put(*((flat_a, 8, k) if k < 8 else (flat_b, 10, 0)), value)
 
     def chunk(g):
         return pl.ds(g * LANES, LANES)
@@ -232,9 +239,11 @@
         acts[g, 64:128, :] = proj_a
         acts[g, 128:192, :] = gate_b
         acts[g, 192:256, :] = proj_b
-        put(18, g, gate_b * proj_b)
-        put(18, 9 + g, gate_a * proj_a)
-    pack(18, send1)
+        put(flat_a, 10, g, gate_b * proj_b)
+        put_left(g, gate_a * proj_a)
+    pack(flat_a, 10, send1a)
+    pack(flat_b, 8, send1b)
+    put(flat_c, 10, 9, jnp.zeros((64, LANES), f32))
 
     @pl.when(own)
     def _():
@@ -244,8 +253,8 @@
     def _():
         pl.semaphore_wait(barrier, 87)
 
-    swap_start(0, send1, recv1, early)
-    swap_start(1, send1, recv1, late)
+    swap_start(0, send1a, recv1a)
+    swap_start(1, send1b, recv1b)
 
     copies = [partner(0, wgo_ref, wgo_other), partner(1, wo_ref, wo_other)]
     for copy in copies:
@@ -266,94 +275,96 @@
     wo = jnp.transpose(wo_t).astype(bf16)
     wo_t = wo_t.astype(bf16)
 
-    swap_wait(0, recv1, early)
+    swap_wait(0, recv1a)
     mine_half = pl.ds(pl.multiple_of(ch * 192, 192), 192)
     other_half = pl.ds(pl.multiple_of((1 - ch) * 192, 192), 192)
-    flat[0:640, :] = recv1[:, early].reshape(640, LANES).astype(f32)
-    right[mine_half, :] = grid_of(10, 0).astype(bf16)
+    unpack(flat_a, 10, recv1a)
+    right[mine_half, :] = grid_of(lambda k: get(flat_a, 10, k)).astype(bf16)
     right_copy = partner(3, right.at[mine_half, :], right.at[mine_half, :])
     right_copy.start()
-    swap_wait(1, recv1, late)
-    unpack(18, recv1)
-    left[...] = grid_of(18, 9).astype(bf16)
+    swap_wait(1, recv1b)
+    unpack(flat_b, 8, recv1b)
+    left[...] = grid_of(get_left).astype(bf16)
     right_copy.wait_recv()
-    put_grid(10, 0, nt(left[...], right[...]))
-    pack(10, send2)
-    swap_start(2, send2, recv2.at[0], ten)
-    swap_wait(2, recv2.at[0], ten)
+    put_grid(lambda k, row: put(flat_c, 10, k, row), nt(left[...], right[...]))
+    pack(flat_c, 10, send2)
+    swap_start(2, send2, recv2.at[0])
+    swap_wait(2, recv2.at[0])
     mixed_copy = partner(4, recv2.at[0], recv2.at[1])
     mixed_copy.start()
     mixed_copy.wait_recv()
 
-    flat_two = []
-    unpack(10, recv2.at[0])
-    first = [get(10, g) for g in range(CHUNKS)]
-    for g in range(CHUNKS):
-        mixn_f = first[g]
-        dfour[0:64, chunk(g)] = mixn_f.astype(bf16)
-    unpack(10, recv2.at[1])
-    for g in range(CHUNKS):
-        mixed = jnp.concatenate([dfour[0:64, chunk(g)].astype(f32), get(10, g)], axis=0)
+    unpack(flat_a, 10, recv2.at[0])
+    unpack(flat_b, 10, recv2.at[1])
+    for g in range(CHUNKS):
+        mixed = jnp.concatenate([get(flat_a, 10, g), get(flat_b, 10, g)], axis=0)
         mean = jnp.mean(mixed, 0, keepdims=True)
         var = jnp.mean(mixed * mixed, 0, keepdims=True) - mean * mean
         inverse = lax.rsqrt(var + epsilon)
         mixed_hat = (mixed - mean) * inverse
         mixed_norm = mixed_hat.astype(bf16)
         mixn[:, chunk(g)] = mixed_norm
-        gate = gate_out[:, chunk(g)]
-        proj_out = nn(wo_t, mixed_norm)
         upstream = jnp.concatenate([cot_t[:, chunk(g)], cot_other[:, chunk(g)]], axis=0).astype(f32)
-        d_proj = (upstream * gate).astype(bf16)
+        d_proj = (upstream * gate_out[:, chunk(g)]).astype(bf16)
+        dproj[:, chunk(g)] = d_proj[0:64]
         d_norm = nn(wo, d_proj)
         d_mean = jnp.mean(d_norm, 0, keepdims=True)
         d_cross = jnp.mean(d_norm * mixed_hat, 0, keepdims=True)
-        d_mixed = inverse[:, :] * (d_norm[0:64] - d_mean - mixed_hat[0:64] * d_cross)
-        acts_flat = d_mixed
-        dmix_rows = acts_flat
-        flat_two.append(dmix_rows)
-        dproj[:, chunk(g)] = d_proj[0:64]
-        gate_mine, proj_mine = gate[0:64], proj_out[0:64]
-        dgate[:, chunk(g)] = (upstream[0:64] * proj_mine * gate_mine * (1.0 - gate_mine)).astype(bf16)
-        updated_ref[chunk(g), :] = jnp.transpose(gate_mine * proj_mine).astype(bf16)
-    for g in range(CHUNKS):
-        put(10, g, flat_two[g])
-    pack(10, send3)
-    swap_start(3, send3, recv3, ten)
+        put(flat_c, 10, g, inverse * (d_norm[0:64] - d_mean - mixed_hat[0:64] * d_cross))
+    pack(flat_c, 10, send3)
+    swap_start(3, send3, recv3)
+    for g in range(CHUNKS):
+        proj_out = nn(wo_t[0:64], mixn[:, chunk(g)])
+        gate = gate_out[0:64, chunk(g)]
+        upstream = cot_t[:, chunk(g)].astype(f32)
+        dgate[:, chunk(g)] = (upstream * proj_out * gate * (1.0 - gate)).astype(bf16)
+        updated_ref[chunk(g), :] = jnp.transpose(gate * proj_out).astype(bf16)
     head_gate = nn(dgate[...], normed[...])
     head_out = nt(dproj[...], mixn[...])
 
-    swap_wait(3, recv3, ten)
-    unpack(10, recv3)
-    d_grid = grid_of(10, 0).astype(bf16)
-    d_right = tn(d_grid, left[...])
-    dr_send[...] = d_right.astype(bf16)
-    dr_copy = partner(5, dr_send.at[other_half, :], dr_recv)
+    swap_wait(3, recv3)
+    unpack(flat_a, 10, recv3)
+    d_grid = grid_of(lambda k: get(flat_a, 10, k))
+    dgrid_t[...] = jnp.transpose(d_grid).astype(bf16)
+    dr_send[...] = nn(dgrid_t[other_half, :], left[...]).astype(bf16)
+    dr_copy = partner(5, dr_send, dr_recv)
     dr_copy.start()
-    put_grid(18, 0, nn(d_grid, right[...]))
-    send4[:, head] = flat[...].astype(bf16).reshape(send4.shape)[:, 0:4]
-    swap_start(4, send4, recv4, head)
+    put_grid(put_d_left, nn(d_grid.astype(bf16), right[...]))
+    pack(flat_a, 8, send4a)
+    swap_start(4, send4a, recv4a)
+    d_right = nn(dgrid_t[mine_half, :], left[...])
     dr_copy.wait_recv()
-    put_grid(18, 9, dr_send[mine_half, :].astype(f32) + dr_recv[...].astype(f32))
-    send4[:, tail] = flat[...].astype(bf16).reshape(send4.shape)[:, 4:9]
-    swap_start(5, send4, recv4, tail)
-    swap_wait(4, recv4, head)
-    swap_wait(5, recv4, tail)
-    unpack(18, recv4)
-    for g in range(CHUNKS):
-        d_left, d_right_g = get(18, g), get(18, 9 + g)
+    put_grid(lambda k, row: put(flat_b, 10, 1 + k, row), d_right + dr_recv[...].astype(f32))
+    pack(flat_b, 10, send4b)
+    swap_start(5, send4b, recv4b)
+    swap_wait(4, recv4a)
+
+    def left_terms(g, d_left):
         gate_a, proj_a = acts[g, 0:64, :], acts[g, 64:128, :]
-        gate_b, proj_b = acts[g, 128:192, :], acts[g, 192:256, :]
         dfour[0:64, chunk(g)] = (d_left * proj_a * gate_a * (1.0 - gate_a)).astype(bf16)
         dfour[64:128, chunk(g)] = (d_left * gate_a).astype(bf16)
+
+    unpack(flat_a, 8, recv4a)
+    for g in range(CHUNKS - 1):
+        left_terms(g, get(flat_a, 8, g))
+    edge_left = nn(dfour[0:128, 0:1024], normed[0:1024, :])
+    swap_wait(5, recv4b)
+    unpack(flat_b, 10, recv4b)
+    left_terms(8, get(flat_b, 10, 0))
+    for g in range(CHUNKS):
+        d_right_g = get(flat_b, 10, 1 + g)
+        gate_b, proj_b = acts[g, 128:192, :], acts[g, 192:256, :]
         dfour[128:192, chunk(g)] = (d_right_g * proj_b * gate_b * (1.0 - gate_b)).astype(bf16)
         dfour[192:256, chunk(g)] = (d_right_g * gate_b).astype(bf16)
-    edge = nn(dfour[...], normed[...])
-
-    for k in range(4):
-        put(6, k, edge[64 * k : 64 * k + 64])
-    put(6, 4, head_gate)
-    put(6, 5, jnp.where(ch == 0, head_out, pltpu.roll(head_out, 64, 1)))
-    pack(6, send5)
+    edge_left += nn(dfour[0:128, 1024:1152], normed[1024:1152, :])
+    edge_right = nn(dfour[128:256, :], normed[...])
+
+    for k in range(2):
+        put(flat_c, 6, k, edge_left[64 * k : 64 * k + 64])
+        put(flat_c, 6, 2 + k, edge_right[64 * k : 64 * k + 64])
+    put(flat_c, 6, 4, head_gate)
+    put(flat_c, 6, 5, jnp.where(ch == 0, head_out, pltpu.roll(head_out, 64, 1)))
+    pack(flat_c, 6, send5)
     e_me, _ = plane_peer(0, 0)
     for dx, dy in plane:
         e, device = plane_peer(dx, dy)
@@ -388,16 +399,12 @@
         group_copy(2, send6, recv6.at[e_me], device).start()
     pltpu.make_async_copy(send6, recv6.at[e_me], grecv_sem.at[2]).start()
     pltpu.make_async_copy(recv6, recv6, grecv_sem.at[2]).wait()
-    flat[0:384, :] = recv6[...].reshape(384, LANES).astype(f32)
+    unpack(flat_c, 6, recv6)
     for k, g_ref in enumerate((g0_ref, g1_ref, g2_ref, g3_ref, g4_ref, g5_ref)):
-        g_ref[...] = get(6, k) * (1.0 / 384)
-
-    swap_drain(0, recv1, early)
-    swap_drain(1, recv1, late)
-    swap_drain(2, recv2.at[0], ten)
-    swap_drain(3, recv3, ten)
-    swap_drain(4, recv4, head)
-    swap_drain(5, recv4, tail)
+        g_ref[...] = get(flat_c, 6, k) * (1.0 / 384)
+
+    for n, dst in enumerate((recv1a, recv1b, recv2.at[0], recv3, recv4a, recv4b)):
+        swap_drain(n, dst)
     pltpu.make_async_copy(recv5.at[pl.ds(0, 15)], recv5.at[pl.ds(0, 15)], gsend_sem.at[0]).wait()
     pltpu.make_async_copy(recvz.at[pl.ds(0, 7)], recvz.at[pl.ds(0, 7)], gsend_sem.at[1]).wait()
     pltpu.make_async_copy(recv6.at[pl.ds(0, 15)], recv6.at[pl.ds(0, 15)], gsend_sem.at[2]).wait()
@@ -418,7 +425,7 @@
     whole = pl.BlockSpec(memory_space=pltpu.VMEM)
     weights = [w.T for w in (w_gate_a, w_proj_a, w_gate_b, w_proj_b, w_gate_out, w_out)]
     vm = pltpu.VMEM
-    big, small = (64, 9, 2, 128), (64, 5, 2, 128)
+    four, five = (64, 4, 2, 128), (64, 5, 2, 128)
     sixteen, eight, one = (16, 24, 128), (8, 24, 128), (24, 128)
     shapes = [jax.ShapeDtypeStruct((PAIRS, 64), bf16)] * 2 + [jax.ShapeDtypeStruct((64, 128), f32)] * 6
     outs = pl.pallas_call(
@@ -433,20 +440,20 @@
             vm((PAIRS, 128), f32),
             vm((PAIRS, 1), f32),
             vm((CHUNKS, 256, 128), f32),
-            vm((PAIRS, 128), f32),
-            vm(big, bf16), vm(big, bf16),
-            vm(small, bf16), vm((2,) + small, bf16),
-            vm(small, bf16), vm(small, bf16),
-            vm(big, bf16), vm(big, bf16),
+            vm((640, 128), f32), vm((640, 128), f32), vm((640, 128), f32),
+            vm(five, bf16), vm(five, bf16), vm(four, bf16), vm(four, bf16),
+            vm(five, bf16), vm((2,) + five, bf16),
+            vm(five, bf16), vm(five, bf16),
+            vm(four, bf16), vm(four, bf16), vm(five, bf16), vm(five, bf16),
             vm(sixteen, bf16), vm(sixteen, bf16),
             vm(one, bf16), vm(eight, bf16),
             vm(one, bf16), vm(sixteen, bf16),
             vm((192, 384), bf16), vm((384, 384), bf16),
-            vm((384, 384), bf16), vm((192, 384), bf16),
+            vm((384, 192), bf16), vm((192, 384), bf16), vm((192, 384), bf16),
             vm((PAIRS, 128), bf16), vm((PAIRS, 128), bf16),
             vm((64, 128), bf16), vm((64, 128), bf16),
             vm((64, PAIRS), bf16), vm((64, PAIRS), bf16),
-            vm((128, PAIRS), f32),
+            vm((128, PAIRS), f32), vm((64, PAIRS), f32),
             vm((64, PAIRS), bf16), vm((64, PAIRS), bf16),
             vm((128, PAIRS), bf16),
             vm((256, PAIRS), bf16),

time: 68.4 us -> 67.2 us (0.982)
  Pallas kernels: 67.7 us -> 66 us
    pallas_call x1, Pallas kernels: 66.7 us -> 65 us  [on_device(): pl.pallas_call(kernel, out_shape=shapes, in_specs=[pl.BlockSpec(memory_sp...]
where the time goes in v3:
time: 67.2 us; the launch traced here: 66.6 us
  Pallas kernels  66 us (98%)
    pallas_call x1, Pallas kernels, on_device(): pl.pallas_call(kernel, out_shape=shapes, in_specs=[pl.BlockSpec(memory_sp...  65 us

profile of v3, /device:TPU:1, one launch (start us, length us, event | category | flops | bytes accessed | tf_op | source)
XLA Modules:
  0.0 66.6 jit_solution(7741735016834663759)
XLA Ops:
  0.6 65.0 %shard_map.143 = (bf16[1152,64]{1,0:T(8,128)(2,1)S(1)}, bf16[1152,64]{1,0:T(8,128)(2,1)S(1)}, f32[64,128]{1,0:T(8,128)S(1)}, f32[64,128]{1,0:T(8,128)S(1)}, f32[...) custom-call(bf16[1152,128]{1,0:T(8,128)(2,1)} %bitcast.16, ...), custom_call_target="tpu_custom_call" | custom-call | tf_op jit(solution)/shard_map/pallas_call | solution.py:431
  65.7 0.9 %shard_map.144 = (bf16[1152,64]{1,0:T(8,128)(2,1)}, bf16[1152,64]{1,0:T(8,128)(2,1)}, f32[64,128]{1,0:T(8,128)}, f32[64,128]{1,0:T(8,128)}, f32[64,128]{1,0:T(8,...) custom-call(bf16[1152,64]{1,0:T(8,128)(2,1)S(1)} %get-tuple-element.24.refs_0_, ...), custom_call_target="tpu_custom_call" | custom-call | tf_op jit(solution)/shard_map/pallas_call | solution.py:471

commit v4 on v3

--- a/solution.py
+++ b/solution.py
@@ -54,11 +54,12 @@
 def kernel(
     pair_hbm, cot_hbm, wga_hbm, wpa_hbm, wgb_hbm, wpb_hbm, wgo_hbm, wo_hbm,
     updated_ref, grad_ref, g0_ref, g1_ref, g2_ref, g3_ref, g4_ref, g5_ref,
-    pair_ref, cot_ref, weights, load_sem, normed, hat, rstd1, acts, flat_a, flat_b, flat_c,
-    send1a, recv1a, send1b, recv1b, send2, recv2, send3, recv3, send4a, recv4a, send4b, recv4b,
+    pair_ref, cot_ref, weights, load_sem, normed, hat, rstd1, acts, flat_a, flat_b, flat_c, pad_four, pad_ten,
+    send1a, recv1a, send1b, recv1b, send2a, recv2a, send2b, recv2b, send3a, recv3a, send3b, recv3b,
+    send4a, recv4a, send4b, recv4b, send4c, recv4c,
     send5, recv5, sendz, recvz, send6, recv6,
-    left, right, dgrid_t, dr_send, dr_recv, df_send, df_recv,
-    wgo_other, wo_other, cot_t, cot_other, gate_out, proj_mine, dproj, dgate, mixn, dfour,
+    left, right, dgrid_t, dr_sum, dr_send, dr_recv, df_send, df_recv,
+    wgo_other, wo_other, cot_t, cot_other, gate_out, dproj, dgate, mixn, dfour,
     send_sem, recv_sem, psend_sem, precv_sem, gsend_sem, grecv_sem,
 ):
     loads = [
@@ -67,9 +68,9 @@
     ]
     loads += [
         pltpu.make_async_copy(pair_hbm.at[rows, :], pair_ref.at[rows, :], load_sem.at[6 + n])
-        for n, rows in enumerate(pl.ds(384 * k, 384) for k in range(3))
+        for n, rows in enumerate(pl.ds(LANES * k, LANES) for k in range(CHUNKS))
     ]
-    loads.append(pltpu.make_async_copy(cot_hbm, cot_ref, load_sem.at[9]))
+    loads.append(pltpu.make_async_copy(cot_hbm, cot_ref, load_sem.at[15]))
     for load in loads:
         load.start()
     wgo_ref, wo_ref = weights.at[pl.ds(256, 64), :], weights.at[pl.ds(320, 64), :]
@@ -187,30 +188,13 @@
     def unpack(flat, rows, src):
         flat[0 : 64 * rows, :] = src[...].reshape(64 * rows, LANES).astype(f32)
 
-    def grid_of(row_of):
-        tiles = [None] * 24
-        for gg in range(3):
-            x = jnp.concatenate([row_of(3 * gg + q) for q in range(3)], axis=1)
-            x = block_transpose(x)
-            for r in range(8):
-                tiles[r * 3 + gg] = x[8 * r : 8 * r + 8]
-        return jnp.concatenate(tiles, axis=0)
-
-    def put_grid(put_row, grid):
-        for gg in range(3):
-            x = jnp.concatenate([grid[8 * (3 * r + gg) : 8 * (3 * r + gg) + 8] for r in range(8)], axis=0)
-            x = block_transpose(x)
-            for q in range(3):
-                put_row(3 * gg + q, x[:, LANES * q : LANES * q + LANES])
-
-    def put_left(k, value):
-        put(*((flat_a, 10, 9) if k == 0 else (flat_b, 8, k - 1)), value)
-
-    def get_left(k):
-        return get(flat_a, 10, 9) if k == 0 else get(flat_b, 8, k - 1)
-
-    def put_d_left(k, value):
-        put(*((flat_a, 8, k) if k < 8 else (flat_b, 10, 0)), value)
+    def rows_at(flat, rows, k):
+        return block_transpose(jnp.concatenate([get(flat, rows, k + q) for q in range(3)], axis=1))
+
+    def put_rows(flat, rows, k, grid):
+        grid = block_transpose(grid)
+        for q in range(3):
+            put(flat, rows, k + q, grid[:, LANES * q : LANES * q + LANES])
 
     def chunk(g):
         return pl.ds(g * LANES, LANES)
@@ -219,8 +203,7 @@
         load.wait()
     w_four = weights[0:256, :]
     for g in range(CHUNKS):
-        if g % 3 == 0:
-            loads[6 + g // 3].wait()
+        loads[6 + g].wait()
         values = pair_ref[chunk(g), :].astype(f32)
         centred = values - jnp.mean(values, -1, keepdims=True)
         spread = jnp.mean(centred * centred, -1, keepdims=True)
@@ -239,11 +222,12 @@
         acts[g, 64:128, :] = proj_a
         acts[g, 128:192, :] = gate_b
         acts[g, 192:256, :] = proj_b
-        put(flat_a, 10, g, gate_b * proj_b)
-        put_left(g, gate_a * proj_a)
-    pack(flat_a, 10, send1a)
-    pack(flat_b, 8, send1b)
-    put(flat_c, 10, 9, jnp.zeros((64, LANES), f32))
+        put(flat_a, 12, g, gate_b * proj_b)
+        put(*((flat_a, 12, 9 + g) if g < 3 else (flat_b, 6, g - 3)), gate_a * proj_a)
+    pack(flat_a, 12, send1a)
+    pack(flat_b, 6, send1b)
+    put(pad_four, 4, 3, jnp.zeros((64, LANES), f32))
+    put(pad_ten, 10, 9, jnp.zeros((64, LANES), f32))
 
     @pl.when(own)
     def _():
@@ -259,7 +243,7 @@
     copies = [partner(0, wgo_ref, wgo_other), partner(1, wo_ref, wo_other)]
     for copy in copies:
         copy.start()
-    loads[9].wait()
+    loads[15].wait()
     for g in range(CHUNKS):
         cot_t[:, chunk(g)] = jnp.transpose(cot_ref[chunk(g), :].astype(f32)).astype(bf16)
     copies.append(partner(2, cot_t, cot_other))
@@ -278,26 +262,29 @@
     swap_wait(0, recv1a)
     mine_half = pl.ds(pl.multiple_of(ch * 192, 192), 192)
     other_half = pl.ds(pl.multiple_of((1 - ch) * 192, 192), 192)
-    unpack(flat_a, 10, recv1a)
-    right[mine_half, :] = grid_of(lambda k: get(flat_a, 10, k)).astype(bf16)
+    unpack(flat_a, 12, recv1a)
+    runs = [rows_at(flat_a, 12, 3 * gg) for gg in range(3)]
+    tiles = [runs[gg][8 * r : 8 * r + 8] for r in range(8) for gg in range(3)]
+    right[mine_half, :] = jnp.concatenate(tiles, axis=0).astype(bf16)
     right_copy = partner(3, right.at[mine_half, :], right.at[mine_half, :])
     right_copy.start()
+    left[0:64, :] = rows_at(flat_a, 12, 9).astype(bf16)
+    right_copy.wait_recv()
+    put_rows(pad_four, 4, 0, nt(left[0:64, :], right[...]))
+    pack(pad_four, 4, send2a)
+    swap_start(2, send2a, recv2a.at[0])
     swap_wait(1, recv1b)
-    unpack(flat_b, 8, recv1b)
-    left[...] = grid_of(get_left).astype(bf16)
-    right_copy.wait_recv()
-    put_grid(lambda k, row: put(flat_c, 10, k, row), nt(left[...], right[...]))
-    pack(flat_c, 10, send2)
-    swap_start(2, send2, recv2.at[0])
-    swap_wait(2, recv2.at[0])
-    mixed_copy = partner(4, recv2.at[0], recv2.at[1])
-    mixed_copy.start()
-    mixed_copy.wait_recv()
-
-    unpack(flat_a, 10, recv2.at[0])
-    unpack(flat_b, 10, recv2.at[1])
-    for g in range(CHUNKS):
-        mixed = jnp.concatenate([get(flat_a, 10, g), get(flat_b, 10, g)], axis=0)
+    unpack(flat_b, 6, recv1b)
+    for k in range(2):
+        left[64 + 64 * k : 128 + 64 * k, :] = rows_at(flat_b, 6, 3 * k).astype(bf16)
+    mixed_b = nt(left[64:192, :], right[...])
+    for k in range(2):
+        put_rows(flat_c, 6, 3 * k, mixed_b[64 * k : 64 * k + 64])
+    pack(flat_c, 6, send2b)
+    swap_start(3, send2b, recv2b.at[0])
+
+    def middle(g, first, second, rows, k, dst):
+        mixed = jnp.concatenate([get(first, rows, k), get(second, rows, k)], axis=0)
         mean = jnp.mean(mixed, 0, keepdims=True)
         var = jnp.mean(mixed * mixed, 0, keepdims=True) - mean * mean
         inverse = lax.rsqrt(var + epsilon)
@@ -310,9 +297,28 @@
         d_norm = nn(wo, d_proj)
         d_mean = jnp.mean(d_norm, 0, keepdims=True)
         d_cross = jnp.mean(d_norm * mixed_hat, 0, keepdims=True)
-        put(flat_c, 10, g, inverse * (d_norm[0:64] - d_mean - mixed_hat[0:64] * d_cross))
-    pack(flat_c, 10, send3)
-    swap_start(3, send3, recv3)
+        put(dst, rows, k, inverse * (d_norm[0:64] - d_mean - mixed_hat[0:64] * d_cross))
+
+    swap_wait(2, recv2a.at[0])
+    mixed_copy_a = partner(4, recv2a.at[0], recv2a.at[1])
+    mixed_copy_a.start()
+    mixed_copy_a.wait_recv()
+    swap_wait(3, recv2b.at[0])
+    mixed_copy_b = partner(8, recv2b.at[0], recv2b.at[1])
+    mixed_copy_b.start()
+    unpack(flat_a, 4, recv2a.at[0])
+    unpack(flat_b, 4, recv2a.at[1])
+    for k in range(3):
+        middle(k, flat_a, flat_b, 4, k, pad_four)
+    pack(pad_four, 4, send3a)
+    swap_start(4, send3a, recv3a)
+    mixed_copy_b.wait_recv()
+    unpack(flat_a, 6, recv2b.at[0])
+    unpack(flat_b, 6, recv2b.at[1])
+    for k in range(6):
+        middle(3 + k, flat_a, flat_b, 6, k, flat_c)
+    pack(flat_c, 6, send3b)
+    swap_start(5, send3b, recv3b)
     for g in range(CHUNKS):
         proj_out = nn(wo_t[0:64], mixn[:, chunk(g)])
         gate = gate_out[0:64, chunk(g)]
@@ -322,41 +328,55 @@
     head_gate = nn(dgate[...], normed[...])
     head_out = nt(dproj[...], mixn[...])
 
-    swap_wait(3, recv3)
-    unpack(flat_a, 10, recv3)
-    d_grid = grid_of(lambda k: get(flat_a, 10, k))
+    swap_wait(4, recv3a)
+    unpack(flat_a, 4, recv3a)
+    d_grid = rows_at(flat_a, 4, 0).astype(bf16)
+    put_rows(pad_four, 4, 0, nn(d_grid, right[...]))
+    pack(pad_four, 4, send4a)
+    swap_start(6, send4a, recv4a)
+    dr_sum[...] = tn(d_grid, left[0:64, :])
+    swap_wait(5, recv3b)
+    unpack(flat_a, 6, recv3b)
+    d_grid = jnp.concatenate([rows_at(flat_a, 6, 3 * k) for k in range(2)], axis=0)
     dgrid_t[...] = jnp.transpose(d_grid).astype(bf16)
-    dr_send[...] = nn(dgrid_t[other_half, :], left[...]).astype(bf16)
+    dr_send[...] = (dr_sum[other_half, :] + nn(dgrid_t[other_half, :], left[64:192, :])).astype(bf16)
     dr_copy = partner(5, dr_send, dr_recv)
     dr_copy.start()
-    put_grid(put_d_left, nn(d_grid.astype(bf16), right[...]))
-    pack(flat_a, 8, send4a)
-    swap_start(4, send4a, recv4a)
-    d_right = nn(dgrid_t[mine_half, :], left[...])
+    d_left = nn(d_grid.astype(bf16), right[...])
+    for k in range(2):
+        put_rows(flat_c, 6, 3 * k, d_left[64 * k : 64 * k + 64])
+    pack(flat_c, 6, send4b)
+    swap_start(7, send4b, recv4b)
+    d_right = dr_sum[mine_half, :] + nn(dgrid_t[mine_half, :], left[64:192, :])
     dr_copy.wait_recv()
-    put_grid(lambda k, row: put(flat_b, 10, 1 + k, row), d_right + dr_recv[...].astype(f32))
-    pack(flat_b, 10, send4b)
-    swap_start(5, send4b, recv4b)
-    swap_wait(4, recv4a)
+    d_right = d_right + dr_recv[...].astype(f32)
+    for gg in range(3):
+        tiles = [d_right[8 * (3 * r + gg) : 8 * (3 * r + gg) + 8] for r in range(8)]
+        put_rows(pad_ten, 10, 3 * gg, jnp.concatenate(tiles, axis=0))
+    pack(pad_ten, 10, send4c)
+    swap_start(8, send4c, recv4c)
 
     def left_terms(g, d_left):
         gate_a, proj_a = acts[g, 0:64, :], acts[g, 64:128, :]
         dfour[0:64, chunk(g)] = (d_left * proj_a * gate_a * (1.0 - gate_a)).astype(bf16)
         dfour[64:128, chunk(g)] = (d_left * gate_a).astype(bf16)
 
-    unpack(flat_a, 8, recv4a)
-    for g in range(CHUNKS - 1):
-        left_terms(g, get(flat_a, 8, g))
-    edge_left = nn(dfour[0:128, 0:1024], normed[0:1024, :])
-    swap_wait(5, recv4b)
-    unpack(flat_b, 10, recv4b)
-    left_terms(8, get(flat_b, 10, 0))
-    for g in range(CHUNKS):
-        d_right_g = get(flat_b, 10, 1 + g)
+    swap_wait(6, recv4a)
+    unpack(flat_a, 4, recv4a)
+    for g in range(3):
+        left_terms(g, get(flat_a, 4, g))
+    swap_wait(7, recv4b)
+    unpack(flat_b, 6, recv4b)
+    for g in range(6):
+        left_terms(3 + g, get(flat_b, 6, g))
+    edge_left = nn(dfour[0:128, :], normed[...])
+    swap_wait(8, recv4c)
+    unpack(pad_ten, 10, recv4c)
+    for g in range(CHUNKS):
+        d_right_g = get(pad_ten, 10, g)
         gate_b, proj_b = acts[g, 128:192, :], acts[g, 192:256, :]
         dfour[128:192, chunk(g)] = (d_right_g * proj_b * gate_b * (1.0 - gate_b)).astype(bf16)
         dfour[192:256, chunk(g)] = (d_right_g * gate_b).astype(bf16)
-    edge_left += nn(dfour[0:128, 1024:1152], normed[1024:1152, :])
     edge_right = nn(dfour[128:256, :], normed[...])
 
     for k in range(2):
@@ -403,12 +423,14 @@
     for k, g_ref in enumerate((g0_ref, g1_ref, g2_ref, g3_ref, g4_ref, g5_ref)):
         g_ref[...] = get(flat_c, 6, k) * (1.0 / 384)
 
-    for n, dst in enumerate((recv1a, recv1b, recv2.at[0], recv3, recv4a, recv4b)):
+    for n, dst in enumerate(
+        (recv1a, recv1b, recv2a.at[0], recv2b.at[0], recv3a, recv3b, recv4a, recv4b, recv4c)
+    ):
         swap_drain(n, dst)
     pltpu.make_async_copy(recv5.at[pl.ds(0, 15)], recv5.at[pl.ds(0, 15)], gsend_sem.at[0]).wait()
     pltpu.make_async_copy(recvz.at[pl.ds(0, 7)], recvz.at[pl.ds(0, 7)], gsend_sem.at[1]).wait()
     pltpu.make_async_copy(recv6.at[pl.ds(0, 15)], recv6.at[pl.ds(0, 15)], gsend_sem.at[2]).wait()
-    for copy in copies + [right_copy, mixed_copy, dr_copy, df_copy]:
+    for copy in copies + [right_copy, mixed_copy_a, mixed_copy_b, dr_copy, df_copy]:
         copy.wait_send()
 
 
@@ -425,7 +447,7 @@
     whole = pl.BlockSpec(memory_space=pltpu.VMEM)
     weights = [w.T for w in (w_gate_a, w_proj_a, w_gate_b, w_proj_b, w_gate_out, w_out)]
     vm = pltpu.VMEM
-    four, five = (64, 4, 2, 128), (64, 5, 2, 128)
+    two, three, five, six = [(64, n, 2, 128) for n in (2, 3, 5, 6)]
     sixteen, eight, one = (16, 24, 128), (8, 24, 128), (24, 128)
     shapes = [jax.ShapeDtypeStruct((PAIRS, 64), bf16)] * 2 + [jax.ShapeDtypeStruct((64, 128), f32)] * 6
     outs = pl.pallas_call(
@@ -435,32 +457,33 @@
         out_specs=[whole] * 8,
         scratch_shapes=[
             vm((PAIRS, 128), bf16), vm((PAIRS, 64), bf16), vm((384, 128), bf16),
-            pltpu.SemaphoreType.DMA((10,)),
+            pltpu.SemaphoreType.DMA((16,)),
             vm((PAIRS, 128), bf16),
             vm((PAIRS, 128), f32),
             vm((PAIRS, 1), f32),
             vm((CHUNKS, 256, 128), f32),
-            vm((640, 128), f32), vm((640, 128), f32), vm((640, 128), f32),
-            vm(five, bf16), vm(five, bf16), vm(four, bf16), vm(four, bf16),
-            vm(five, bf16), vm((2,) + five, bf16),
-            vm(five, bf16), vm(five, bf16),
-            vm(four, bf16), vm(four, bf16), vm(five, bf16), vm(five, bf16),
+            vm((768, 128), f32), vm((768, 128), f32), vm((384, 128), f32),
+            vm((256, 128), f32), vm((640, 128), f32),
+            vm(six, bf16), vm(six, bf16), vm(three, bf16), vm(three, bf16),
+            vm(two, bf16), vm((2,) + two, bf16), vm(three, bf16), vm((2,) + three, bf16),
+            vm(two, bf16), vm(two, bf16), vm(three, bf16), vm(three, bf16),
+            vm(two, bf16), vm(two, bf16), vm(three, bf16), vm(three, bf16), vm(five, bf16), vm(five, bf16),
             vm(sixteen, bf16), vm(sixteen, bf16),
             vm(one, bf16), vm(eight, bf16),
             vm(one, bf16), vm(sixteen, bf16),
             vm((192, 384), bf16), vm((384, 384), bf16),
-            vm((384, 192), bf16), vm((192, 384), bf16), vm((192, 384), bf16),
+            vm((384, 128), bf16), vm((384, 384), f32), vm((192, 384), bf16), vm((192, 384), bf16),
             vm((PAIRS, 128), bf16), vm((PAIRS, 128), bf16),
             vm((64, 128), bf16), vm((64, 128), bf16),
             vm((64, PAIRS), bf16), vm((64, PAIRS), bf16),
-            vm((128, PAIRS), f32), vm((64, PAIRS), f32),
+            vm((128, PAIRS), f32),
             vm((64, PAIRS), bf16), vm((64, PAIRS), bf16),
             vm((128, PAIRS), bf16),
             vm((256, PAIRS), bf16),
-            pltpu.SemaphoreType.DMA((6,)),
-            pltpu.SemaphoreType.DMA((6,)),
-            pltpu.SemaphoreType.DMA((8,)),
-            pltpu.SemaphoreType.DMA((8,)),
+            pltpu.SemaphoreType.DMA((9,)),
+            pltpu.SemaphoreType.DMA((9,)),
+            pltpu.SemaphoreType.DMA((9,)),
+            pltpu.SemaphoreType.DMA((9,)),
             pltpu.SemaphoreType.DMA((3,)),
             pltpu.SemaphoreType.DMA((3,)),
         ],

time: 67.2 us -> 66 us (0.982)
  Pallas kernels: 66 us -> 64.4 us
    pallas_call x1, Pallas kernels: 65 us -> 63.5 us  [on_device(): pl.pallas_call(kernel, out_shape=shapes, in_specs=[pl.BlockSpec(memory_sp...]
where the time goes in v4:
time: 66 us; the launch traced here: 65.1 us
  Pallas kernels  64.4 us (98%)
    pallas_call x1, Pallas kernels, on_device(): pl.pallas_call(kernel, out_shape=shapes, in_specs=[pl.BlockSpec(memory_sp...  63.5 us

profile of v4, /device:TPU:1, one launch (start us, length us, event | category | flops | bytes accessed | tf_op | source)
XLA Modules:
  0.0 65.1 jit_solution(13240101529971379505)
XLA Ops:
  0.6 63.5 %shard_map.143 = (bf16[1152,64]{1,0:T(8,128)(2,1)S(1)}, bf16[1152,64]{1,0:T(8,128)(2,1)S(1)}, f32[64,128]{1,0:T(8,128)S(1)}, f32[64,128]{1,0:T(8,128)S(1)}, f32[...) custom-call(bf16[1152,128]{1,0:T(8,128)(2,1)} %bitcast.16, ...), custom_call_target="tpu_custom_call" | custom-call | tf_op jit(solution)/shard_map/pallas_call | solution.py:453
  64.1 0.9 %shard_map.144 = (bf16[1152,64]{1,0:T(8,128)(2,1)}, bf16[1152,64]{1,0:T(8,128)(2,1)}, f32[64,128]{1,0:T(8,128)}, f32[64,128]{1,0:T(8,128)}, f32[64,128]{1,0:T(8,...) custom-call(bf16[1152,64]{1,0:T(8,128)(2,1)S(1)} %get-tuple-element.24.refs_0_, ...), custom_call_target="tpu_custom_call" | custom-call | tf_op jit(solution)/shard_map/pallas_call | solution.py:494

commit v5 on v4

--- a/solution.py
+++ b/solution.py
@@ -37,25 +37,24 @@
 )
 
 
-def block_transpose(x):
-    groups = x.shape[0] // 8
-    x = x.reshape(groups, 8, 384)
-    row = lax.broadcasted_iota(jnp.int32, x.shape, 1)
-    part = lax.broadcasted_iota(jnp.int32, x.shape, 2) // 48
+def trade(arrays):
+    arrays = list(arrays)
+    part = lax.broadcasted_iota(jnp.int32, arrays[0].shape, 1) // 48
     for bit in (1, 2, 4):
-        low = (row & bit) == 0
-        same = low == ((part & bit) == 0)
-        up = pltpu.roll(pltpu.roll(x, bit, 1), 384 - 48 * bit, 2)
-        down = pltpu.roll(pltpu.roll(x, 8 - bit, 1), 48 * bit, 2)
-        x = jnp.where(same, x, jnp.where(low, down, up))
-    return x.reshape(groups * 8, 384)
+        high = (part & bit) != 0
+        for c in range(8):
+            if c & bit == 0:
+                a, b = arrays[c], arrays[c | bit]
+                arrays[c] = jnp.where(high, pltpu.roll(b, 48 * bit, 1), a)
+                arrays[c | bit] = jnp.where(high, b, pltpu.roll(a, 384 - 48 * bit, 1))
+    return arrays
 
 
 def kernel(
     pair_hbm, cot_hbm, wga_hbm, wpa_hbm, wgb_hbm, wpb_hbm, wgo_hbm, wo_hbm,
     updated_ref, grad_ref, g0_ref, g1_ref, g2_ref, g3_ref, g4_ref, g5_ref,
-    pair_ref, cot_ref, weights, load_sem, normed, hat, rstd1, acts, flat_a, flat_b, flat_c, pad_four, pad_ten,
-    send1a, recv1a, send1b, recv1b, send2a, recv2a, send2b, recv2b, send3a, recv3a, send3b, recv3b,
+    pair_ref, cot_ref, weights, load_sem, normed, hat, rstd1, acts, flat_a, flat_b, flat_c, pad_four, pad_ten, grid,
+    send1a, recv1a, send1b, recv1b, send1c, recv1c, send2a, recv2a, send2b, recv2b, send3a, recv3a, send3b, recv3b,
     send4a, recv4a, send4b, recv4b, send4c, recv4c,
     send5, recv5, sendz, recvz, send6, recv6,
     left, right, dgrid_t, dr_sum, dr_send, dr_recv, df_send, df_recv,
@@ -63,14 +62,14 @@
     send_sem, recv_sem, psend_sem, precv_sem, gsend_sem, grecv_sem,
 ):
     loads = [
-        pltpu.make_async_copy(src, weights.at[pl.ds(64 * n, 64), :], load_sem.at[n])
+        pltpu.make_async_copy(pair_hbm.at[rows, :], pair_ref.at[rows, :], load_sem.at[n])
+        for n, rows in enumerate(pl.ds(384 * k, 384) for k in range(3))
+    ]
+    loads += [
+        pltpu.make_async_copy(src, weights.at[pl.ds(64 * n, 64), :], load_sem.at[3 + n])
         for n, src in enumerate((wga_hbm, wpa_hbm, wgb_hbm, wpb_hbm, wgo_hbm, wo_hbm))
     ]
-    loads += [
-        pltpu.make_async_copy(pair_hbm.at[rows, :], pair_ref.at[rows, :], load_sem.at[6 + n])
-        for n, rows in enumerate(pl.ds(LANES * k, LANES) for k in range(CHUNKS))
-    ]
-    loads.append(pltpu.make_async_copy(cot_hbm, cot_ref, load_sem.at[15]))
+    loads.append(pltpu.make_async_copy(cot_hbm, cot_ref, load_sem.at[9]))
     for load in loads:
         load.start()
     wgo_ref, wo_ref = weights.at[pl.ds(256, 64), :], weights.at[pl.ds(320, 64), :]
@@ -188,22 +187,33 @@
     def unpack(flat, rows, src):
         flat[0 : 64 * rows, :] = src[...].reshape(64 * rows, LANES).astype(f32)
 
+    def run_of(three):
+        def piece(flat, rows, k, c):
+            return flat[pl.ds(c * rows + k, 8, stride=8 * rows), :]
+
+        return trade([jnp.concatenate([piece(*at, c) for at in three], axis=1) for c in range(8)])
+
     def rows_at(flat, rows, k):
-        return block_transpose(jnp.concatenate([get(flat, rows, k + q) for q in range(3)], axis=1))
+        return jnp.concatenate(run_of([(flat, rows, k + q) for q in range(3)]), axis=0)
+
+    def put_run(three, arrays):
+        for c, array in enumerate(trade(arrays)):
+            for q, (flat, rows, k) in enumerate(three):
+                flat[pl.ds(c * rows + k, 8, stride=8 * rows), :] = array[:, LANES * q : LANES * q + LANES]
+
+    def eight(grid):
+        return [grid[8 * m : 8 * m + 8] for m in range(8)]
 
     def put_rows(flat, rows, k, grid):
-        grid = block_transpose(grid)
-        for q in range(3):
-            put(flat, rows, k + q, grid[:, LANES * q : LANES * q + LANES])
+        put_run([(flat, rows, k + q) for q in range(3)], eight(grid))
 
     def chunk(g):
         return pl.ds(g * LANES, LANES)
 
-    for load in loads[0:6]:
+    for load in loads[0:9]:
         load.wait()
     w_four = weights[0:256, :]
     for g in range(CHUNKS):
-        loads[6 + g].wait()
         values = pair_ref[chunk(g), :].astype(f32)
         centred = values - jnp.mean(values, -1, keepdims=True)
         spread = jnp.mean(centred * centred, -1, keepdims=True)
@@ -222,12 +232,12 @@
         acts[g, 64:128, :] = proj_a
         acts[g, 128:192, :] = gate_b
         acts[g, 192:256, :] = proj_b
-        put(flat_a, 12, g, gate_b * proj_b)
-        put(*((flat_a, 12, 9 + g) if g < 3 else (flat_b, 6, g - 3)), gate_a * proj_a)
-    pack(flat_a, 12, send1a)
+        put(flat_a, 10, g, gate_b * proj_b)
+        put(*((flat_a, 10, 9) if g == 0 else (pad_ten, 2, g - 1) if g < 3 else (flat_b, 6, g - 3)), gate_a * proj_a)
+    pack(flat_a, 10, send1a)
+    pack(pad_ten, 2, send1c)
     pack(flat_b, 6, send1b)
     put(pad_four, 4, 3, jnp.zeros((64, LANES), f32))
-    put(pad_ten, 10, 9, jnp.zeros((64, LANES), f32))
 
     @pl.when(own)
     def _():
@@ -238,12 +248,13 @@
         pl.semaphore_wait(barrier, 87)
 
     swap_start(0, send1a, recv1a)
+    swap_start(9, send1c, recv1c)
     swap_start(1, send1b, recv1b)
 
     copies = [partner(0, wgo_ref, wgo_other), partner(1, wo_ref, wo_other)]
     for copy in copies:
         copy.start()
-    loads[15].wait()
+    loads[9].wait()
     for g in range(CHUNKS):
         cot_t[:, chunk(g)] = jnp.transpose(cot_ref[chunk(g), :].astype(f32)).astype(bf16)
     copies.append(partner(2, cot_t, cot_other))
@@ -262,13 +273,18 @@
     swap_wait(0, recv1a)
     mine_half = pl.ds(pl.multiple_of(ch * 192, 192), 192)
     other_half = pl.ds(pl.multiple_of((1 - ch) * 192, 192), 192)
-    unpack(flat_a, 12, recv1a)
-    runs = [rows_at(flat_a, 12, 3 * gg) for gg in range(3)]
-    tiles = [runs[gg][8 * r : 8 * r + 8] for r in range(8) for gg in range(3)]
-    right[mine_half, :] = jnp.concatenate(tiles, axis=0).astype(bf16)
+    unpack(flat_a, 10, recv1a)
+    for gg in range(3):
+        for m, array in enumerate(run_of([(flat_a, 10, 3 * gg + q) for q in range(3)])):
+            for q in range(3):
+                grid[q, pl.ds(8 * gg + m, 8, stride=24), :] = array[:, LANES * q : LANES * q + LANES]
+    for q in range(3):
+        right[mine_half, LANES * q : LANES * q + LANES] = grid[q].astype(bf16)
     right_copy = partner(3, right.at[mine_half, :], right.at[mine_half, :])
     right_copy.start()
-    left[0:64, :] = rows_at(flat_a, 12, 9).astype(bf16)
+    swap_wait(9, recv1c)
+    unpack(flat_c, 2, recv1c)
+    left[0:64, :] = jnp.concatenate(run_of([(flat_a, 10, 9), (flat_c, 2, 0), (flat_c, 2, 1)]), axis=0).astype(bf16)
     right_copy.wait_recv()
     put_rows(pad_four, 4, 0, nt(left[0:64, :], right[...]))
     pack(pad_four, 4, send2a)
@@ -331,8 +347,8 @@
     swap_wait(4, recv3a)
     unpack(flat_a, 4, recv3a)
     d_grid = rows_at(flat_a, 4, 0).astype(bf16)
-    put_rows(pad_four, 4, 0, nn(d_grid, right[...]))
-    pack(pad_four, 4, send4a)
+    put_run([(flat_b, 2, 0), (flat_b, 2, 1), (flat_c, 6, 0)], eight(nn(d_grid, right[...])))
+    pack(flat_b, 2, send4a)
     swap_start(6, send4a, recv4a)
     dr_sum[...] = tn(d_grid, left[0:64, :])
     swap_wait(5, recv3b)
@@ -343,16 +359,21 @@
     dr_copy = partner(5, dr_send, dr_recv)
     dr_copy.start()
     d_left = nn(d_grid.astype(bf16), right[...])
-    for k in range(2):
-        put_rows(flat_c, 6, 3 * k, d_left[64 * k : 64 * k + 64])
+    put_rows(flat_c, 6, 1, d_left[0:64])
+    put_run([(flat_c, 6, 4), (flat_c, 6, 5), (pad_ten, 10, 0)], eight(d_left[64:128]))
     pack(flat_c, 6, send4b)
     swap_start(7, send4b, recv4b)
     d_right = dr_sum[mine_half, :] + nn(dgrid_t[mine_half, :], left[64:192, :])
     dr_copy.wait_recv()
     d_right = d_right + dr_recv[...].astype(f32)
+    for q in range(3):
+        grid[q] = d_right[:, LANES * q : LANES * q + LANES]
     for gg in range(3):
-        tiles = [d_right[8 * (3 * r + gg) : 8 * (3 * r + gg) + 8] for r in range(8)]
-        put_rows(pad_ten, 10, 3 * gg, jnp.concatenate(tiles, axis=0))
+        arrays = [
+            jnp.concatenate([grid[q, pl.ds(8 * gg + m, 8, stride=24), :] for q in range(3)], axis=1)
+            for m in range(8)
+        ]
+        put_run([(pad_ten, 10, 1 + 3 * gg + q) for q in range(3)], arrays)
     pack(pad_ten, 10, send4c)
     swap_start(8, send4c, recv4c)
 
@@ -362,21 +383,23 @@
         dfour[64:128, chunk(g)] = (d_left * gate_a).astype(bf16)
 
     swap_wait(6, recv4a)
-    unpack(flat_a, 4, recv4a)
-    for g in range(3):
-        left_terms(g, get(flat_a, 4, g))
+    unpack(flat_a, 2, recv4a)
+    for g in range(2):
+        left_terms(g, get(flat_a, 2, g))
     swap_wait(7, recv4b)
     unpack(flat_b, 6, recv4b)
     for g in range(6):
-        left_terms(3 + g, get(flat_b, 6, g))
-    edge_left = nn(dfour[0:128, :], normed[...])
+        left_terms(2 + g, get(flat_b, 6, g))
+    edge_left = nn(dfour[0:128, 0:1024], normed[0:1024, :])
     swap_wait(8, recv4c)
     unpack(pad_ten, 10, recv4c)
-    for g in range(CHUNKS):
-        d_right_g = get(pad_ten, 10, g)
+    left_terms(8, get(pad_ten, 10, 0))
+    for g in range(CHUNKS):
+        d_right_g = get(pad_ten, 10, 1 + g)
         gate_b, proj_b = acts[g, 128:192, :], acts[g, 192:256, :]
         dfour[128:192, chunk(g)] = (d_right_g * proj_b * gate_b * (1.0 - gate_b)).astype(bf16)
         dfour[192:256, chunk(g)] = (d_right_g * gate_b).astype(bf16)
+    edge_left += nn(dfour[0:128, 1024:1152], normed[1024:1152, :])
     edge_right = nn(dfour[128:256, :], normed[...])
 
     for k in range(2):
@@ -424,7 +447,7 @@
         g_ref[...] = get(flat_c, 6, k) * (1.0 / 384)
 
     for n, dst in enumerate(
-        (recv1a, recv1b, recv2a.at[0], recv2b.at[0], recv3a, recv3b, recv4a, recv4b, recv4c)
+        (recv1a, recv1b, recv2a.at[0], recv2b.at[0], recv3a, recv3b, recv4a, recv4b, recv4c, recv1c)
     ):
         swap_drain(n, dst)
     pltpu.make_async_copy(recv5.at[pl.ds(0, 15)], recv5.at[pl.ds(0, 15)], gsend_sem.at[0]).wait()
@@ -447,8 +470,8 @@
     whole = pl.BlockSpec(memory_space=pltpu.VMEM)
     weights = [w.T for w in (w_gate_a, w_proj_a, w_gate_b, w_proj_b, w_gate_out, w_out)]
     vm = pltpu.VMEM
-    two, three, five, six = [(64, n, 2, 128) for n in (2, 3, 5, 6)]
-    sixteen, eight, one = (16, 24, 128), (8, 24, 128), (24, 128)
+    one, two, three, five = [(64, n, 2, 128) for n in (1, 2, 3, 5)]
+    sixteen, eight, block = (16, 24, 128), (8, 24, 128), (24, 128)
     shapes = [jax.ShapeDtypeStruct((PAIRS, 64), bf16)] * 2 + [jax.ShapeDtypeStruct((64, 128), f32)] * 6
     outs = pl.pallas_call(
         kernel,
@@ -457,20 +480,20 @@
         out_specs=[whole] * 8,
         scratch_shapes=[
             vm((PAIRS, 128), bf16), vm((PAIRS, 64), bf16), vm((384, 128), bf16),
-            pltpu.SemaphoreType.DMA((16,)),
+            pltpu.SemaphoreType.DMA((10,)),
             vm((PAIRS, 128), bf16),
             vm((PAIRS, 128), f32),
             vm((PAIRS, 1), f32),
             vm((CHUNKS, 256, 128), f32),
             vm((768, 128), f32), vm((768, 128), f32), vm((384, 128), f32),
-            vm((256, 128), f32), vm((640, 128), f32),
-            vm(six, bf16), vm(six, bf16), vm(three, bf16), vm(three, bf16),
+            vm((256, 128), f32), vm((640, 128), f32), vm((3, 192, 128), f32),
+            vm(five, bf16), vm(five, bf16), vm(three, bf16), vm(three, bf16), vm(one, bf16), vm(one, bf16),
             vm(two, bf16), vm((2,) + two, bf16), vm(three, bf16), vm((2,) + three, bf16),
             vm(two, bf16), vm(two, bf16), vm(three, bf16), vm(three, bf16),
-            vm(two, bf16), vm(two, bf16), vm(three, bf16), vm(three, bf16), vm(five, bf16), vm(five, bf16),
+            vm(one, bf16), vm(one, bf16), vm(three, bf16), vm(three, bf16), vm(five, bf16), vm(five, bf16),
             vm(sixteen, bf16), vm(sixteen, bf16),
-            vm(one, bf16), vm(eight, bf16),
-            vm(one, bf16), vm(sixteen, bf16),
+            vm(block, bf16), vm(eight, bf16),
+            vm(block, bf16), vm(sixteen, bf16),
             vm((192, 384), bf16), vm((384, 384), bf16),
             vm((384, 128), bf16), vm((384, 384), f32), vm((192, 384), bf16), vm((192, 384), bf16),
             vm((PAIRS, 128), bf16), vm((PAIRS, 128), bf16),
@@ -480,8 +503,8 @@
             vm((64, PAIRS), bf16), vm((64, PAIRS), bf16),
             vm((128, PAIRS), bf16),
             vm((256, PAIRS), bf16),
-            pltpu.SemaphoreType.DMA((9,)),
-            pltpu.SemaphoreType.DMA((9,)),
+            pltpu.SemaphoreType.DMA((10,)),
+            pltpu.SemaphoreType.DMA((10,)),
             pltpu.SemaphoreType.DMA((9,)),
             pltpu.SemaphoreType.DMA((9,)),
             pltpu.SemaphoreType.DMA((3,)),

time: 66 us -> 65.8 us (level); the launches traced: 65.1 us -> 65.6 us
  no operation moved by 1% of the time
where the time goes in v5:
time: 65.8 us; the launch traced here: 65.6 us
  Pallas kernels  65 us (99%)
    pallas_call x1, Pallas kernels, on_device(): pl.pallas_call(kernel, out_shape=shapes, in_specs=[pl.BlockSpec(memory_sp...  64 us

profile of v5, /device:TPU:1, one launch (start us, length us, event | category | flops | bytes accessed | tf_op | source)
XLA Modules:
  0.0 65.6 jit_solution(7608515043769708235)
XLA Ops:
  0.6 64.0 %shard_map.143 = (bf16[1152,64]{1,0:T(8,128)(2,1)S(1)}, bf16[1152,64]{1,0:T(8,128)(2,1)S(1)}, f32[64,128]{1,0:T(8,128)S(1)}, f32[64,128]{1,0:T(8,128)S(1)}, f32[...) custom-call(bf16[1152,128]{1,0:T(8,128)(2,1)} %bitcast.16, ...), custom_call_target="tpu_custom_call" | custom-call | tf_op jit(solution)/shard_map/pallas_call | solution.py:476
  64.7 0.9 %shard_map.144 = (bf16[1152,64]{1,0:T(8,128)(2,1)}, bf16[1152,64]{1,0:T(8,128)(2,1)}, f32[64,128]{1,0:T(8,128)}, f32[64,128]{1,0:T(8,128)}, f32[64,128]{1,0:T(8,...) custom-call(bf16[1152,64]{1,0:T(8,128)(2,1)S(1)} %get-tuple-element.24.refs_0_, ...), custom_call_target="tpu_custom_call" | custom-call | tf_op jit(solution)/shard_map/pallas_call | solution.py:517

commit v6 on v5

--- a/solution.py
+++ b/solution.py
@@ -248,8 +248,6 @@
         pl.semaphore_wait(barrier, 87)
 
     swap_start(0, send1a, recv1a)
-    swap_start(9, send1c, recv1c)
-    swap_start(1, send1b, recv1b)
 
     copies = [partner(0, wgo_ref, wgo_other), partner(1, wo_ref, wo_other)]
     for copy in copies:
@@ -270,6 +268,8 @@
     wo = jnp.transpose(wo_t).astype(bf16)
     wo_t = wo_t.astype(bf16)
 
+    swap_start(9, send1c, recv1c)
+    swap_start(1, send1b, recv1b)
     swap_wait(0, recv1a)
     mine_half = pl.ds(pl.multiple_of(ch * 192, 192), 192)
     other_half = pl.ds(pl.multiple_of((1 - ch) * 192, 192), 192)
@@ -319,15 +319,15 @@
     mixed_copy_a = partner(4, recv2a.at[0], recv2a.at[1])
     mixed_copy_a.start()
     mixed_copy_a.wait_recv()
-    swap_wait(3, recv2b.at[0])
-    mixed_copy_b = partner(8, recv2b.at[0], recv2b.at[1])
-    mixed_copy_b.start()
     unpack(flat_a, 4, recv2a.at[0])
     unpack(flat_b, 4, recv2a.at[1])
     for k in range(3):
         middle(k, flat_a, flat_b, 4, k, pad_four)
     pack(pad_four, 4, send3a)
     swap_start(4, send3a, recv3a)
+    swap_wait(3, recv2b.at[0])
+    mixed_copy_b = partner(8, recv2b.at[0], recv2b.at[1])
+    mixed_copy_b.start()
     mixed_copy_b.wait_recv()
     unpack(flat_a, 6, recv2b.at[0])
     unpack(flat_b, 6, recv2b.at[1])

time: 65.8 us -> 65.7 us (level); the launches traced: 65.6 us -> 64.5 us
  Pallas kernels: 65 us -> 63.9 us
    pallas_call x1, Pallas kernels: 64 us -> 62.9 us  [on_device(): pl.pallas_call(kernel, out_shape=shapes, in_specs=[pl.BlockSpec(memory_sp...]
where the time goes in v6:
time: 65.7 us; the launch traced here: 64.5 us
  Pallas kernels  63.9 us (97%)
    pallas_call x1, Pallas kernels, on_device(): pl.pallas_call(kernel, out_shape=shapes, in_specs=[pl.BlockSpec(memory_sp...  62.9 us

profile of v6, /device:TPU:1, one launch (start us, length us, event | category | flops | bytes accessed | tf_op | source)
XLA Modules:
  0.0 64.5 jit_solution(10802526545442174596)
XLA Ops:
  0.6 62.9 %shard_map.143 = (bf16[1152,64]{1,0:T(8,128)(2,1)S(1)}, bf16[1152,64]{1,0:T(8,128)(2,1)S(1)}, f32[64,128]{1,0:T(8,128)S(1)}, f32[64,128]{1,0:T(8,128)S(1)}, f32[...) custom-call(bf16[1152,128]{1,0:T(8,128)(2,1)} %bitcast.16, ...), custom_call_target="tpu_custom_call" | custom-call | tf_op jit(solution)/shard_map/pallas_call | solution.py:476
  63.6 0.9 %shard_map.144 = (bf16[1152,64]{1,0:T(8,128)(2,1)}, bf16[1152,64]{1,0:T(8,128)(2,1)}, f32[64,128]{1,0:T(8,128)}, f32[64,128]{1,0:T(8,128)}, f32[64,128]{1,0:T(8,...) custom-call(bf16[1152,64]{1,0:T(8,128)(2,1)S(1)} %get-tuple-element.24.refs_0_, ...), custom_call_target="tpu_custom_call" | custom-call | tf_op jit(solution)/shard_map/pallas_call | solution.py:517

commit v7 on v6

--- a/solution.py
+++ b/solution.py
@@ -70,8 +70,6 @@
         for n, src in enumerate((wga_hbm, wpa_hbm, wgb_hbm, wpb_hbm, wgo_hbm, wo_hbm))
     ]
     loads.append(pltpu.make_async_copy(cot_hbm, cot_ref, load_sem.at[9]))
-    for load in loads:
-        load.start()
     wgo_ref, wo_ref = weights.at[pl.ds(256, 64), :], weights.at[pl.ds(320, 64), :]
 
     row, col, ch = lax.axis_index("row"), lax.axis_index("col"), lax.axis_index("ch")
@@ -116,6 +114,8 @@
     def _():
         greet(peer(slot))
 
+    for load in loads:
+        load.start()
     for dx, dy in plane:
         greet(plane_peer(dx, dy)[1])
     for dz in (4, 3, 5, 2, 6, 1, 7):

time: 65.7 us -> 65.7 us (level)
  no operation moved by 1% of the time
where the time goes in v7:
time: 65.7 us; the launch traced here: 64.4 us
  Pallas kernels  63.7 us (97%)
    pallas_call x1, Pallas kernels, on_device(): pl.pallas_call(kernel, out_shape=shapes, in_specs=[pl.BlockSpec(memory_sp...  62.8 us

profile of v7, /device:TPU:1, one launch (start us, length us, event | category | flops | bytes accessed | tf_op | source)
XLA Modules:
  0.0 64.4 jit_solution(13212731503253760237)
XLA Ops:
  0.6 62.8 %shard_map.143 = (bf16[1152,64]{1,0:T(8,128)(2,1)S(1)}, bf16[1152,64]{1,0:T(8,128)(2,1)S(1)}, f32[64,128]{1,0:T(8,128)S(1)}, f32[64,128]{1,0:T(8,128)S(1)}, f32[...) custom-call(bf16[1152,128]{1,0:T(8,128)(2,1)} %bitcast.16, ...), custom_call_target="tpu_custom_call" | custom-call | tf_op jit(solution)/shard_map/pallas_call | solution.py:476
  63.5 0.9 %shard_map.144 = (bf16[1152,64]{1,0:T(8,128)(2,1)}, bf16[1152,64]{1,0:T(8,128)(2,1)}, f32[64,128]{1,0:T(8,128)}, f32[64,128]{1,0:T(8,128)}, f32[64,128]{1,0:T(8,...) custom-call(bf16[1152,64]{1,0:T(8,128)(2,1)S(1)} %get-tuple-element.24.refs_0_, ...), custom_call_target="tpu_custom_call" | custom-call | tf_op jit(solution)/shard_map/pallas_call | solution.py:517
